TPU v7x, 768 devices: a whole 4x8x12 slice. The times are simulated.
768 devices in a mesh: replica: 48 (over x_lo, z, core), fsdp: 16 (over y, x_hi).
Axes of the slice: x: 4 (x_hi: 2, x_lo: 2; x = x_hi * 2 + x_lo), y: 8, z: 12, core: 2. Of those that a mesh axis runs over, the one named last changes fastest.
Arguments:
- tokens: bfloat16 [98304, 8192], P(('replica', 'fsdp')), may hold values from -6 to 6
- target: bfloat16 [98304, 512], P(('replica', 'fsdp')), may hold values from -6 to 6
- weight: bfloat16 [48, 8192, 512], P('replica', 'fsdp'), may hold values from -6 to 6
- pseudo: float32 [48, 8192, 512], P('replica', 'fsdp'), may hold values from -6 to 6
- global_frag: float32 [8192, 512], P('fsdp'), may hold values from -6 to 6
- momentum: float32 [8192, 512], P('fsdp'), may hold values from -2 to 2
Outputs:
- new_weight: bfloat16 [48, 8192, 512], P('replica', 'fsdp')
- residual: bfloat16 [98304, 512], P(('replica', 'fsdp'))
- new_global: float32 [8192, 512], P('fsdp')
- new_momentum: float32 [8192, 512], P('fsdp')
All inputs are finite; a program needn't handle non-finite values.
Results may differ from a plain program's by a relative error of at most 0.013.
Values may be sent and summed in bfloat16 or wider, within the bound.
No kernel may reach another device: no remote copies, remote signals or barrier semaphores. Data moves between devices by JAX's collectives and lax.ppermute only.
A program may use at most 64 MiB of HBM per device.

v0:
```python
import jax
import jax.numpy as jnp
from jax import lax
from jax.sharding import Mesh
from jax.sharding import PartitionSpec as P

FSDP = ("fsdp_0", "fsdp_1")
REPLICA_FSDP = ("replica", "fsdp_0", "fsdp_1")


inner_rate = 1.0
outer_rate = 0.7
nesterov_coef = 0.9
merge_share = 0.5


def gathered_by_axis(value, axes, dim):
    if not axes:
        return value
    nearer = lax.all_gather(value, axes[-1], axis=dim, tiled=True)
    return gathered_by_axis(nearer, axes[:-1], dim)


def shards(tokens, target, weight, pseudo, global_frag, momentum):
    model_width = tokens.shape[1]
    key_scale = model_width ** (-0.5)
    weight_rows = weight[0]
    columns = lax.all_to_all(tokens, FSDP, split_axis=1, concat_axis=0, tiled=True)
    token_block = columns
    keys_own = lax.psum_scatter(
        (jnp.dot(token_block, weight_rows, preferred_element_type=jnp.float32) * key_scale).astype(
            jnp.bfloat16
        ),
        FSDP,
        scatter_dimension=0,
        tiled=True,
    ).astype(jnp.float32)
    residual_own = (keys_own - target.astype(jnp.float32)).astype(jnp.bfloat16)
    token_block = columns
    gradient = (
        lax.dot_general(
            token_block,
            gathered_by_axis(residual_own, FSDP, 0),
            (((0,), (0,)), ((), ())),
            preferred_element_type=jnp.float32,
        )
        * key_scale
    )
    stepped = weight_rows.astype(jnp.float32) - inner_rate * gradient
    summed = lax.psum(pseudo[0], "replica")
    averaged = summed / lax.axis_size("replica")
    new_momentum = nesterov_coef * momentum + averaged
    new_global = global_frag - outer_rate * (averaged + nesterov_coef * new_momentum)
    new_weight = (merge_share * stepped + (1.0 - merge_share) * new_global).astype(jnp.bfloat16)
    return (new_weight[None], residual_own, new_global, new_momentum)


def solution(mesh):
    split = Mesh(mesh.devices.reshape(mesh.shape["replica"], 8, 2), ("replica", "fsdp_0", "fsdp_1"))
    placed = (
        P(REPLICA_FSDP, None),
        P(REPLICA_FSDP, None),
        P("replica", FSDP, None),
        P("replica", FSDP, None),
        P(FSDP, None),
        P(FSDP, None),
    )
    return jax.shard_map(
        shards,
        mesh=split,
        in_specs=placed,
        out_specs=(P("replica", FSDP, None), P(REPLICA_FSDP, None), P(FSDP, None), P(FSDP, None)),
        check_vma=False,
    )
```

profile of v0, /device:TPU:1, one launch (start us, length us, event | category | flops | bytes accessed | tf_op | source)
XLA Modules:
  0.0 436.8 jit_solution(12678033639051016683)
XLA Ops:
  8.0 0.0 reduce-scatter.2.cloned.1.call-start
  8.0 3.2 copy.25
  11.3 58.3 %all_to_all.19 = bf16[128,16,512]{0,2,1:T(8,128)(2,1)} all-to-all(bf16[128,16,512]{0,2,1:T(8,128)(2,1)S(1)} %bitcast.29), channel_id=1, replica_groups=mesh['replica'=48,'fsdp_0'=8,'fsdp_1'=2] {'fsdp_0','fsdp_1'}, dimensions={1} | all-to-all | bytes 4194304 | tf_op jit(solution)/shard_map/all_to_all | solution.py:28
  69.5 0.0 copy-start.3
  69.5 2.9 copy.26
  72.5 0.0 copy-done.3
  72.5 2.6 multiply_convert_fusion
  75.1 0.0 copy-start
  75.1 0.0 reduce-scatter.2.cloned.1.call-update
  75.1 0.0 copy-start.4
  75.1 0.0 all-reduce.2.cloned.1.call-start
  75.2 1.1 copy-done
  76.3 1.3 copy.27
  77.6 0.0 all-reduce.2.cloned.1.call-update
  77.6 0.0 all-gather.2.cloned.1.call-start
  77.7 217.7 %reduce-scatter.2.cloned.1.call-done = bf16[128,512]{1,0:T(8,128)(2,1)} async-done(((bf16[2048,512]{1,0:T(8,128)(2,1)}), bf16[128,512]{1,0:T(8,128)(2,1)}) %reduce-scatter.2.cloned.1.call-update) | async-done | bytes 131088 | tf_op jit(solution)/shard_map/reduce_scatter | solution.py:30
  295.4 0.0 copy-done.4
  295.4 0.9 subtract_convert_fusion
  296.4 0.0 copy-start.2
  296.4 6.2 %all_gather.6 = bf16[256,512]{1,0:T(8,128)(2,1)} all-gather(bf16[128,512]{1,0:T(8,128)(2,1)S(1)} %subtract_convert_fusion), channel_id=1, replica_groups=mesh['replica'=48,'fsdp_0'=8,'fsdp_1'=2] {'fsdp_1'}, dimensions={0}, use_global_device_ids=true | all-gather | bytes 393216 | tf_op jit(solution)/shard_map/all_gather | solution.py:20
  302.5 0.0 all-gather.2.cloned.1.call-update
  302.6 2.0 copy.24
  304.6 0.0 copy-done.1
  304.6 1.3 copy.28
  305.9 2.6 copy.29
  308.5 0.0 copy-done.2
  308.5 107.9 %all-reduce.2.cloned.1.call-done = f32[512,512]{0,1:T(8,128)} async-done(((f32[512,512]{0,1:T(8,128)}), f32[512,512]{0,1:T(8,128)}) %all-reduce.2.cloned.1.call-update) | async-done | bytes 1048592 | tf_op jit(solution)/shard_map/psum | solution.py:50
  416.4 3.2 multiply_add_fusion
  419.6 1.3 copy.31
  420.9 2.5 copy.32
  423.5 3.8 fusion.5
  427.3 2.0 copy.30
  (2 shorter events, 0.0 us)
Async XLA Ops:
  8.0 287.4 %reduce-scatter.2.cloned.1.call-start = ((), (), s32[]{:S(2)}) async-start(), calls=%async_computation.2 | async-start | bytes 2228224 | tf_op jit(solution)/shard_map/reduce_scatter | solution.py:30
  69.5 2.9 copy-start.3
  75.1 1.2 copy-start
  75.1 220.3 %copy-start.4 = (bf16[128,512]{1,0:T(8,128)(2,1)S(1)}, bf16[128,512]{1,0:T(8,128)(2,1)}, u32[]{:S(2)}) copy-start(bf16[128,512]{1,0:T(8,128)(2,1)} %param.7) | copy-start | bytes 393220
  75.1 341.3 %all-reduce.2.cloned.1.call-start = ((), (), s32[]{:S(2)}) async-start(), calls=%async_computation.4 | async-start | bytes 2097152 | tf_op jit(solution)/shard_map/psum | solution.py:50
  77.6 227.0 %copy-start.1 = (f32[512,512]{1,0:T(8,128)S(1)}, f32[512,512]{1,0:T(8,128)}, u32[]{:S(2)}) copy-start(f32[512,512]{1,0:T(8,128)} %param.11) | copy-start | bytes 3145732
  77.6 345.8 %all-gather.2.cloned.1.call-start = ((), (), s32[]{:S(2)}) async-start(), calls=%async_computation.3 | async-start | bytes 2359296 | tf_op jit(solution)/shard_map/all_gather | solution.py:20
  296.4 12.1 %copy-start.2 = (bf16[128,512]{1,0:T(8,128)(2,1)}, bf16[128,512]{1,0:T(8,128)(2,1)S(1)}, u32[]{:S(2)}) copy-start(bf16[128,512]{1,0:T(8,128)(2,1)S(1)} %subtract_convert_fusion) | copy-start | bytes 393220
Sparse Core Ops, SparseCore 0:
  75.2 220.1 reduce-scatter.1
  302.7 45.6 all-gather.1
Sparse Core Ops, SparseCore 1:
  79.4 337.0 all-reduce.1
where the time goes:
time: 437 us
  waiting for transfers between devices  326 us (75%)
  blocking collectives  64.4 us (15%)
  local copies, waits for them, and re-layouts  20.4 us (5%)
  between operations  15.5 us (4%)
  matrix products  6.41 us (1%)
    reduce_scatter x1, waiting for transfers between devices, shards(): lax.psum_scatter((jnp.dot(token_block, weight_rows, preferred_element_typ...  218 us
    psum x1, waiting for transfers between devices, shards(): summed = lax.psum(pseudo[0], 'replica')  108 us
    all_to_all x1, blocking collectives, shards(): lax.all_to_all(tokens, FSDP, split_axis=1, concat_axis=0, tiled=True)  58.3 us
    unnamed x18, local copies, waits for them, and re-layouts  17.5 us
  transfers between devices with their start and end apart: 3, of which 2 were waited for; matrix products, arithmetic and copies ran while one was open for 3% of the time, Pallas kernels for 0%

commit v1 on v0

v1 whole, which is shorter than its diff:
```python
import functools

import jax
import jax.numpy as jnp
from jax import lax
from jax.experimental import pallas as pl
from jax.experimental.pallas import tpu as pltpu
from jax.sharding import Mesh
from jax.sharding import PartitionSpec as P


Y = ("yh", "yl")
FSDP = ("yh", "yl", "xh")
REPLICA = ("xl", "zh", "zl", "core")
SWAP = [(0, 1), (1, 0)]
VMEM_LIMIT = 16 * 2**20

inner_rate = 1.0
outer_rate = 0.7
nesterov_coef = 0.9
merge_share = 0.5


def halved(total, axis, dim):
    me = lax.axis_index(axis)
    sent = lax.dynamic_index_in_dim(total, 1 - me, dim, keepdims=False).astype(jnp.bfloat16)
    got = lax.ppermute(sent, axis, SWAP)
    return lax.dynamic_index_in_dim(total, me, dim, keepdims=False) + got.astype(jnp.float32)


def replica_mean(pseudo):
    rows, columns = pseudo.shape
    replicas = lax.axis_size(REPLICA)
    total = pseudo.reshape(2, 2, 2, rows // 8, columns)
    total = halved(total, "core", 2)
    total = halved(total, "xl", 0)
    total = halved(total, "zl", 0)
    parts = lax.all_gather(total.astype(jnp.bfloat16), "zh", axis=0)
    mean = (jnp.sum(parts.astype(jnp.float32), axis=0) / replicas).astype(jnp.bfloat16)
    return lax.all_gather(mean, ("xl", "zl", "core"), axis=0, tiled=True).astype(jnp.float32)


def split_kernel(tokens_ref, out_ref):
    out_ref[0] = tokens_ref[...]


def split_columns(tokens, parts):
    rows, columns = tokens.shape
    width = columns // parts
    return pl.pallas_call(
        split_kernel,
        grid=(parts,),
        in_specs=[pl.BlockSpec((rows, width), lambda i: (0, i))],
        out_specs=pl.BlockSpec((1, rows, width), lambda i: (i, 0, 0)),
        out_shape=jax.ShapeDtypeStruct((parts, rows, width), tokens.dtype),
        name="split_columns",
    )(tokens)


def partial_kernel(scale, place_ref, x_ref, own_ref, other_ref, out_ref):
    width = own_ref.shape[0]
    low, high = x_ref[0, :, :width], x_ref[0, :, width:]

    def emit(low_rows, high_rows):
        total = jnp.dot(low, low_rows[...], preferred_element_type=jnp.float32)
        total += jnp.dot(high, high_rows[...], preferred_element_type=jnp.float32)
        out_ref[0] = (total * scale).astype(out_ref.dtype)

    @pl.when(place_ref[1] == 0)
    def _():
        emit(own_ref, other_ref)

    @pl.when(place_ref[1] != 0)
    def _():
        emit(other_ref, own_ref)


def partial_keys(place, blocks, own_rows, other_rows, scale):
    parts, rows, columns = blocks.shape
    width, key_width = own_rows.shape
    whole = pl.BlockSpec((width, key_width), lambda i, place: (0, 0))
    return pl.pallas_call(
        functools.partial(partial_kernel, scale),
        grid_spec=pltpu.PrefetchScalarGridSpec(
            num_scalar_prefetch=1,
            grid=(parts,),
            in_specs=[pl.BlockSpec((1, rows, columns), lambda i, place: (i, 0, 0)), whole, whole],
            out_specs=pl.BlockSpec((1, rows, key_width), lambda i, place: (i, 0, 0)),
        ),
        out_shape=jax.ShapeDtypeStruct((parts, rows, key_width), jnp.bfloat16),
        cost_estimate=pl.CostEstimate(
            flops=2 * parts * rows * columns * key_width,
            bytes_accessed=2 * parts * rows * (columns + key_width) + 4 * width * key_width,
            transcendentals=0,
        ),
        compiler_params=pltpu.CompilerParams(vmem_limit_bytes=VMEM_LIMIT),
        name="partial_keys",
    )(place, blocks, own_rows, other_rows)


def turn_kernel(place_ref, near_ref, far_ref, send_near, keep_near, send_far, keep_far):
    width = send_near.shape[0]

    def emit(keep, send):
        for source, kept, sent in ((near_ref, keep_near, send_near), (far_ref, keep_far, send_far)):
            kept[...] = source[0, :, keep * width : (keep + 1) * width].T
            sent[...] = source[0, :, send * width : (send + 1) * width].T

    @pl.when(place_ref[1] == 0)
    def _():
        emit(0, 1)

    @pl.when(place_ref[1] != 0)
    def _():
        emit(1, 0)


def turned(place, blocks):
    parts, rows, columns = blocks.shape
    width = columns // 2
    out = jax.ShapeDtypeStruct((width, parts // 2 * rows), blocks.dtype)
    return pl.pallas_call(
        turn_kernel,
        grid_spec=pltpu.PrefetchScalarGridSpec(
            num_scalar_prefetch=1,
            grid=(parts // 2,),
            in_specs=[
                pl.BlockSpec((1, rows, columns), lambda k, place: (2 * k + place[0], 0, 0)),
                pl.BlockSpec((1, rows, columns), lambda k, place: (2 * k + 1 - place[0], 0, 0)),
            ],
            out_specs=[pl.BlockSpec((width, rows), lambda k, place: (0, k))] * 4,
        ),
        out_shape=[out] * 4,
        cost_estimate=pl.CostEstimate(flops=0, bytes_accessed=4 * parts * rows * columns, transcendentals=0),
        compiler_params=pltpu.CompilerParams(vmem_limit_bytes=VMEM_LIMIT),
        name="turn",
    )(place, blocks, blocks)


def residual_kernel(pieces_ref, target_ref, out_ref):
    total = pieces_ref[0].astype(jnp.float32)
    for f in range(1, pieces_ref.shape[0]):
        total += pieces_ref[f].astype(jnp.float32)
    out_ref[...] = (total - target_ref[...].astype(jnp.float32)).astype(out_ref.dtype)


def residual_of(pieces, target):
    rows, key_width = target.shape
    parts = pieces.shape[0]
    step = rows // 4
    return pl.pallas_call(
        residual_kernel,
        grid=(4,),
        in_specs=[
            pl.BlockSpec((parts, step, key_width), lambda i: (0, i, 0)),
            pl.BlockSpec((step, key_width), lambda i: (i, 0)),
        ],
        out_specs=pl.BlockSpec((step, key_width), lambda i: (i, 0)),
        out_shape=jax.ShapeDtypeStruct((rows, key_width), jnp.bfloat16),
        compiler_params=pltpu.CompilerParams(vmem_limit_bytes=VMEM_LIMIT),
        name="residual",
    )(pieces, target)


def shards(tokens, target, weight, pseudo, global_frag, momentum):
    _, model_width = tokens.shape
    key_scale = model_width ** (-0.5)
    weight_rows = weight[0]
    _, key_width = weight_rows.shape
    place = jnp.stack([lax.axis_index("yl"), lax.axis_index("xh")]).astype(jnp.int32)

    blocks = lax.all_to_all(split_columns(tokens, lax.axis_size(Y)), Y, 0, 0, tiled=True)

    other_rows = lax.ppermute(weight_rows, "xh", SWAP)
    averaged = replica_mean(pseudo[0])

    partial = partial_keys(place, blocks, weight_rows, other_rows, key_scale)
    pieces = lax.all_to_all(partial, Y, 0, 0, tiled=True)

    send_near, keep_near, send_far, keep_far = turned(place, blocks)
    new_momentum = nesterov_coef * momentum + averaged
    new_global = global_frag - outer_rate * (averaged + nesterov_coef * new_momentum)
    merged = merge_share * weight_rows.astype(jnp.float32) + (1.0 - merge_share) * new_global
    new_momentum, new_global, merged = lax.optimization_barrier((new_momentum, new_global, merged))

    residual = residual_of(pieces, target)
    near = lax.all_gather(residual, "yh", axis=0, tiled=True)
    cut = key_width // 2
    far = []
    for c in range(2):
        far.append(lax.ppermute(near[:, c * cut : (c + 1) * cut], "yl", SWAP))

    def product(block, values):
        return jnp.dot(block, values, preferred_element_type=jnp.float32)

    sent_near = product(send_near, near)
    kept_near = merged - (merge_share * inner_rate * key_scale) * product(keep_near, near)
    sent_near, kept_near = lax.optimization_barrier((sent_near, kept_near))
    new_weight = []
    for c in range(2):
        part = slice(c * cut, (c + 1) * cut)
        sent = ((sent_near[:, part] + product(send_far, far[c])) * key_scale).astype(jnp.bfloat16)
        got = lax.ppermute(sent, "xh", SWAP)
        kept = kept_near[:, part] - (merge_share * inner_rate * key_scale) * product(keep_far, far[c])
        kept = lax.optimization_barrier(kept)
        new_weight.append((kept - (merge_share * inner_rate) * got.astype(jnp.float32)).astype(jnp.bfloat16))
    return (jnp.concatenate(new_weight, axis=1)[None], residual, new_global, new_momentum)


def solution(mesh):
    split = Mesh(mesh.devices.reshape(2, 6, 2, 2, 4, 2, 2), REPLICA + FSDP)
    rows = P(REPLICA + FSDP, None)
    per_replica = P(REPLICA, FSDP, None)
    shared = P(FSDP, None)
    return jax.shard_map(
        shards,
        mesh=split,
        in_specs=(rows, rows, per_replica, per_replica, shared, shared),
        out_specs=(per_replica, rows, shared, shared),
        check_vma=False,
    )
```

time: 437 us -> 183 us (0.42)
  waiting for transfers between devices: 326 us -> 41.6 us
  starting transfers between devices: 0.12 us -> 45.7 us
  between operations: 15.5 us -> 0.9 us
  local copies, waits for them, and re-layouts: 20.4 us -> 6 us
  Pallas kernels: 0 us -> 13.6 us
    reduce_scatter x1 -> x0, waiting for transfers between devices: 218 us -> none  [shards(): lax.psum_scatter((jnp.dot(token_block, weight_rows, preferred_element_typ...]
    psum x1 -> x0, waiting for transfers between devices: 108 us -> none  [shards(): summed = lax.psum(pseudo[0], 'replica')]
    all_to_all x1 -> x0, blocking collectives: 58.3 us -> none  [shards(): lax.all_to_all(tokens, FSDP, split_axis=1, concat_axis=0, tiled=True)]
    all_gather x1 -> x3, blocking collectives: 6.16 us -> 63.4 us  [the longest x1 27.2 us: replica_mean(): parts = lax.all_gather(total.astype(jnp.bfloat16), 'zh', axis=0)]
    ppermute x0 -> x8, starting transfers between devices: none -> 32.8 us  [the longest x3 18.2 us: halved(): got = lax.ppermute(sent, axis, SWAP)]
    ppermute x0 -> x8, waiting for transfers between devices: none -> 22.4 us  [the longest x1 10 us: shards(): other_rows = lax.ppermute(weight_rows, 'xh', SWAP)]
    all_to_all x0 -> x2, waiting for transfers between devices: none -> 19.2 us  [the longest x1 19.2 us: shards(): lax.all_to_all(split_columns(tokens, lax.axis_size(Y)), Y, 0, 0, tiled=True)]
    unnamed x18 -> x26, local copies, waits for them, and re-layouts: 17.5 us -> 3.2 us
  transfers between devices with their start and end apart: 3 -> 10, of which waited for: 2 -> 6; matrix products, arithmetic and copies ran while one was open for 3% -> 6% of each run, Pallas kernels for 0% -> 4%
where the time goes in v1:
time: 183 us; the launch traced here: 181 us
  blocking collectives  63.4 us (35%)
  starting transfers between devices  45.7 us (25%)
  waiting for transfers between devices  41.6 us (23%)
  Pallas kernels  13.6 us (7%)
  other arithmetic  7.38 us (4%)
  local copies, waits for them, and re-layouts  6 us (3%)
  matrix products  2.06 us (1%)
    all_gather x1, blocking collectives, replica_mean(): parts = lax.all_gather(total.astype(jnp.bfloat16), 'zh', axis=0)  27.2 us
    all_to_all x1, waiting for transfers between devices, shards(): lax.all_to_all(split_columns(tokens, lax.axis_size(Y)), Y, 0, 0, tiled=True)  19.2 us
    all_gather x1, blocking collectives, replica_mean(): lax.all_gather(mean, ('xl', 'zl', 'core'), axis=0, tiled=True)  18.2 us
    ppermute x3, starting transfers between devices, halved(): got = lax.ppermute(sent, axis, SWAP)  18.2 us
    all_gather x1, blocking collectives, shards(): near = lax.all_gather(residual, 'yh', axis=0, tiled=True)  17.9 us
    ppermute x1, waiting for transfers between devices, shards(): other_rows = lax.ppermute(weight_rows, 'xh', SWAP)  10 us
    all_to_all x1, starting transfers between devices, shards(): lax.all_to_all(split_columns(tokens, lax.axis_size(Y)), Y, 0, 0, tiled=True)  7.77 us
    ppermute x2, starting transfers between devices, shards(): got = lax.ppermute(sent, 'xh', SWAP)  7.28 us
  transfers between devices with their start and end apart: 10, of which 6 were waited for; matrix products, arithmetic and copies ran while one was open for 6% of the time, Pallas kernels for 4%

profile of v1, /device:TPU:1, one launch (start us, length us, event | category | flops | bytes accessed | tf_op | source)
XLA Modules:
  0.0 180.7 jit_solution(16342114949675623690)
XLA Ops:
  0.6 5.6 %split_columns.1 = bf16[8,128,1024]{2,1,0:T(8,128)(2,1)} custom-call(bf16[128,8192]{1,0:T(8,128)(2,1)} %tokens_ref.1), custom_call_target="tpu_custom_call" | custom-call | tf_op jit(solution)/shard_map/split_columns/pallas_call | solution.py:50
  6.3 7.8 %all-to-all-start = ((bf16[8,128,1024]{2,1,0:T(8,128)(2,1)}), bf16[8,128,1024]{2,1,0:T(8,128)(2,1)S(1)}, u32[]{:S(2)}, u32[]{:S(2)}) async-start(bf16[8,128,1024]{2,1,0:T(8,128)(2,1)} %split_columns.1), calls=%async_computation | async-start | bytes 4194304 | tf_op jit(solution)/shard_map/all_to_all | solution.py:172
  14.0 1.8 fusion.9
  15.8 8.4 %collective-permute-start.1 = (bf16[2,2,64,512]{3,2,1,0:T(8,128)(2,1)}, bf16[2,2,64,512]{3,2,1,0:T(8,128)(2,1)S(1)}, u32[]{:S(2)}, u32[]{:S(2)}) collective-permute-start(bf16[2,2,64,512]{3,2,1,0:T(8,128)(2,1)} %fusion.9), channel_id=1, source_target_pairs={{0,16},{16,0},{1,17},{17,1},{2,18},{18,2},{3,19},{19,3},{4,20},{20... | collective-permute-start | bytes 786440 | tf_op jit(solution)/shard_map/ppermute | solution.py:27
  24.2 1.9 %collective-permute-start = (bf16[512,512]{1,0:T(8,128)(2,1)S(1)}, bf16[512,512]{1,0:T(8,128)(2,1)S(1)}, u32[]{:S(2)}, u32[]{:S(2)}) collective-permute-start(bf16[512,512]{1,0:T(8,128)(2,1)S(1)} %bitcast.35), channel_id=1, source_target_pairs={{0,1},{1,0},{2,3},{3,2},{4,5},{5,4},{6,7},{7,6},{8,9},{9,8},{10,11... | collective-permute-start | bytes 1572872 | tf_op jit(solution)/shard_map/ppermute | solution.py:174
  26.2 1.9 %bitcast_add_fusion = f32[2,2,64,512]{3,2,1,0:T(8,128)} fusion(bf16[2,2,64,512]{3,2,1,0:T(8,128)(2,1)S(1)} %collective-permute-done.1, f32[2,2,2,64,512]{4,3,2,1,0:T(8,128)} %bitcast.39, s32[]{:T(128)S(6)} %select_n.21), kind=kLoop, calls=%fused_computation.19 | loop fusion | flops 262144 | bytes 1310724 | tf_op jit(solution)/shard_map/add | solution.py:28
  28.1 1.0 fusion.10
  29.1 1.9 %collective-permute-start.2 = (bf16[2,64,512]{2,1,0:T(8,128)(2,1)S(1)}, bf16[2,64,512]{2,1,0:T(8,128)(2,1)}, u32[]{:S(2)}, u32[]{:S(2)}) collective-permute-start(bf16[2,64,512]{2,1,0:T(8,128)(2,1)S(1)} %fusion.10), channel_id=1, source_target_pairs={{0,384},{384,0},{1,385},{385,1},{2,386},{386,2},{3,387},{387,3},{4... | collective-permute-start | bytes 393224 | tf_op jit(solution)/shard_map/ppermute | solution.py:27
  31.0 10.0 %collective-permute-done.other_ref = bf16[512,512]{1,0:T(8,128)(2,1)S(1)} collective-permute-done((bf16[512,512]{1,0:T(8,128)(2,1)S(1)}, bf16[512,512]{1,0:T(8,128)(2,1)S(1)}, u32[]{:S(2)}, u32[]{:S(2)}) %collective-permute-start) | collective-permute-done | bytes 524320 | tf_op jit(solution)/shard_map/ppermute | solution.py:174
  41.0 19.2 %all-to-all-done.near_ref.far_ref.x_ref = bf16[8,128,1024]{2,1,0:T(8,128)(2,1)S(1)} async-done(((bf16[8,128,1024]{2,1,0:T(8,128)(2,1)}), bf16[8,128,1024]{2,1,0:T(8,128)(2,1)S(1)}, u32[]{:S(2)}, u32[]{:S(2)}) %all-to-all-start) | async-done | bytes 2097184 | tf_op jit(solution)/shard_map/all_to_all | solution.py:172
  60.2 4.8 %partial_keys.1 = bf16[8,128,512]{2,1,0:T(8,128)(2,1)} custom-call(s32[2]{0:T(128)S(1)} %pad_add_fusion.place_ref, bf16[8,128,1024]{2,1,0:T(8,128)(2,1)S(1)} %all-to-all-done.near_ref.far_ref.x_ref, bf16[512,512]{1,0:T(8,128)(2,1)S(1)} %bitcast.36, bf16[512,512]{1,0:T(8,128)(2,1)S(1)} %collective-permute-done.other_ref), custom_call_target="tpu_custom_call" | custom-call | flops 1073741824 | bytes 4194304 | tf_op jit(solution)/shard_map/partial_keys/pallas_call | solution.py:82
  65.0 5.1 %all-to-all-start.1 = ((bf16[8,128,512]{2,1,0:T(8,128)(2,1)}), bf16[8,128,512]{2,1,0:T(8,128)(2,1)S(1)}, u32[]{:S(2)}, u32[]{:S(2)}) async-start(bf16[8,128,512]{2,1,0:T(8,128)(2,1)} %partial_keys.1), calls=%async_computation.1 | async-start | bytes 2097152 | tf_op jit(solution)/shard_map/all_to_all | solution.py:178
  70.1 1.1 bitcast_add_fusion.1
  71.2 7.9 %collective-permute-start.3 = (bf16[64,512]{1,0:T(8,128)(2,1)S(1)}, bf16[64,512]{1,0:T(8,128)(2,1)S(1)}, u32[]{:S(2)}, u32[]{:S(2)}) collective-permute-start(bf16[64,512]{1,0:T(8,128)(2,1)S(1)} %fusion.12), channel_id=1, source_target_pairs={{0,32},{32,0},{1,33},{33,1},{2,34},{34,2},{3,35},{35,3},{4,36},{36... | collective-permute-start | bytes 196616 | tf_op jit(solution)/shard_map/ppermute | solution.py:27
  79.2 1.9 %collective-permute-done.3 = bf16[64,512]{1,0:T(8,128)(2,1)S(1)} collective-permute-done((bf16[64,512]{1,0:T(8,128)(2,1)S(1)}, bf16[64,512]{1,0:T(8,128)(2,1)S(1)}, u32[]{:S(2)}, u32[]{:S(2)}) %collective-permute-start.3) | collective-permute-done | bytes 65568 | tf_op jit(solution)/shard_map/ppermute | solution.py:27
  81.1 27.2 %all-gather = bf16[384,512]{1,0:T(8,128)(2,1)S(1)} all-gather(bf16[64,512]{1,0:T(8,128)(2,1)S(1)} %fusion.11), channel_id=2, replica_groups=mesh['xl'=2,'zh'=6,'zl'=2,'core'=2,'yh'=4,'yl'=2,'xh'=2] {'zh'}, dimensions={0}, use_global_device_ids=true | all-gather | bytes 458752 | tf_op jit(solution)/shard_map/all_gather | solution.py:38
  108.4 18.2 %all_gather.15 = bf16[512,512]{1,0:T(8,128)(2,1)S(1)} all-gather(bf16[64,512]{1,0:T(8,128)(2,1)S(1)} %multiply_convert_fusion), channel_id=1, replica_groups=mesh['xl'=2,'zh'=6,'zl'=2,'core'=2,'yh'=4,'yl'=2,'xh'=2] {'xl','zl','core'}, dimensions={0}, use_global_device_ids=true | all-gather | bytes 589824 | tf_op jit(solution)/shard_map/all_gather | solution.py:40
  126.7 3.2 %add_multiply_fusion = (f32[512,512]{1,0:T(8,128)}, f32[512,512]{1,0:T(8,128)}, f32[512,512]{1,0:T(8,128)}) fusion(bf16[1,512,512]{2,1,0:T(8,128)(2,1)S(1)} %copy-done.1, f32[512,512]{1,0:T(8,128)S(1)} %copy-done.12, f32[512,512]{1,0:T(8,128)} %param.11, bf16[512,512]{1,0:T(8,128)(2,1)S(1)} %all_gather.15), kind=kLoop, calls=%fused_computation.16 | loop fusion | flops 2621440 | bytes 6291456 | tf_op jit(solution)/shard_map/add | solution.py:183
  129.9 1.8 turn.1
  132.5 0.8 copy-done.4
  133.3 0.8 copy-done.6
  134.1 0.8 copy-done.8
  134.9 1.5 residual.1
  136.4 17.9 %all_gather.12 = bf16[512,512]{1,0:T(8,128)(2,1)S(1)} all-gather(bf16[128,512]{1,0:T(8,128)(2,1)} %residual.1), channel_id=1, replica_groups=mesh['xl'=2,'zh'=6,'zl'=2,'core'=2,'yh'=4,'yl'=2,'xh'=2] {'yh'}, dimensions={0}, use_global_device_ids=true | all-gather | bytes 655360 | tf_op jit(solution)/shard_map/all_gather | solution.py:187
  154.3 2.1 %collective-permute-start.4 = (bf16[512,256]{1,0:T(8,128)(2,1)S(1)}, bf16[512,256]{1,0:T(8,128)(2,1)S(1)}, u32[]{:S(2)}, u32[]{:S(2)}) collective-permute-start(bf16[512,256]{1,0:T(8,128)(2,1)S(1)} %get-tuple-element.25), channel_id=1, source_target_pairs={{0,2},{2,0},{1,3},{3,1},{4,6},{6,4},{5,7},{7,5},{8,10},{10,8},{9,1... | collective-permute-start | bytes 786440 | tf_op jit(solution)/shard_map/ppermute | solution.py:191
  156.4 3.4 %collective-permute-start.6 = (bf16[512,256]{1,0:T(8,128)(2,1)S(1)}, bf16[512,256]{1,0:T(8,128)(2,1)S(1)}, u32[]{:S(2)}, u32[]{:S(2)}) collective-permute-start(bf16[512,256]{1,0:T(8,128)(2,1)S(1)} %get-tuple-element.26), channel_id=1, source_target_pairs={{0,2},{2,0},{1,3},{3,1},{4,6},{6,4},{5,7},{7,5},{8,10},{10,8},{9,1... | collective-permute-start | bytes 786440 | tf_op jit(solution)/shard_map/ppermute | solution.py:191
  160.7 1.9 %collective-permute-done.4 = bf16[512,256]{1,0:T(8,128)(2,1)S(1)} collective-permute-done((bf16[512,256]{1,0:T(8,128)(2,1)S(1)}, bf16[512,256]{1,0:T(8,128)(2,1)S(1)}, u32[]{:S(2)}, u32[]{:S(2)}) %collective-permute-start.4) | collective-permute-done | bytes 262176 | tf_op jit(solution)/shard_map/ppermute | solution.py:191
  162.9 3.6 %collective-permute-start.5 = (bf16[512,256]{1,0:T(8,128)(2,1)S(1)}, bf16[512,256]{1,0:T(8,128)(2,1)S(1)}, u32[]{:S(2)}, u32[]{:S(2)}) collective-permute-start(bf16[512,256]{1,0:T(8,128)(2,1)S(1)} %fusion.5), channel_id=1, source_target_pairs={{0,1},{1,0},{2,3},{3,2},{4,5},{5,4},{6,7},{7,6},{8,9},{9,8},{10,11... | collective-permute-start | bytes 786440 | tf_op jit(solution)/shard_map/ppermute | solution.py:203
  166.6 1.7 collective-permute-done.6
  168.5 3.6 %collective-permute-start.7 = (bf16[512,256]{1,0:T(8,128)(2,1)S(1)}, bf16[512,256]{1,0:T(8,128)(2,1)S(1)}, u32[]{:S(2)}, u32[]{:S(2)}) collective-permute-start(bf16[512,256]{1,0:T(8,128)(2,1)S(1)} %fusion.6), channel_id=1, source_target_pairs={{0,1},{1,0},{2,3},{3,2},{4,5},{5,4},{6,7},{7,6},{8,9},{9,8},{10,11... | collective-permute-start | bytes 786440 | tf_op jit(solution)/shard_map/ppermute | solution.py:203
  172.9 6.8 %collective-permute-done.7 = bf16[512,256]{1,0:T(8,128)(2,1)S(1)} collective-permute-done((bf16[512,256]{1,0:T(8,128)(2,1)S(1)}, bf16[512,256]{1,0:T(8,128)(2,1)S(1)}, u32[]{:S(2)}, u32[]{:S(2)}) %collective-permute-start.7) | collective-permute-done | bytes 262176 | tf_op jit(solution)/shard_map/ppermute | solution.py:203
  179.8 0.8 maximum_bitcast_fusion
  (41 shorter events, 3.3 us)
Async XLA Ops:
  6.3 17.9 %copy-start = (bf16[1,512,512]{2,1,0:T(8,128)(2,1)S(1)}, bf16[1,512,512]{2,1,0:T(8,128)(2,1)}, u32[]{:S(2)}) copy-start(bf16[1,512,512]{2,1,0:T(8,128)(2,1)} %param.8) | copy-start | bytes 1572868
  6.3 54.0 %all-to-all-start = ((bf16[8,128,1024]{2,1,0:T(8,128)(2,1)}), bf16[8,128,1024]{2,1,0:T(8,128)(2,1)S(1)}, u32[]{:S(2)}, u32[]{:S(2)}) async-start(bf16[8,128,1024]{2,1,0:T(8,128)(2,1)} %split_columns.1), calls=%async_computation | async-start | bytes 4194304 | tf_op jit(solution)/shard_map/all_to_all | solution.py:172
  15.8 10.4 %collective-permute-start.1 = (bf16[2,2,64,512]{3,2,1,0:T(8,128)(2,1)}, bf16[2,2,64,512]{3,2,1,0:T(8,128)(2,1)S(1)}, u32[]{:S(2)}, u32[]{:S(2)}) collective-permute-start(bf16[2,2,64,512]{3,2,1,0:T(8,128)(2,1)} %fusion.9), channel_id=1, source_target_pairs={{0,16},{16,0},{1,17},{17,1},{2,18},{18,2},{3,19},{19,3},{4,20},{20... | collective-permute-start | bytes 786440 | tf_op jit(solution)/shard_map/ppermute | solution.py:27
  24.2 16.9 %collective-permute-start = (bf16[512,512]{1,0:T(8,128)(2,1)S(1)}, bf16[512,512]{1,0:T(8,128)(2,1)S(1)}, u32[]{:S(2)}, u32[]{:S(2)}) collective-permute-start(bf16[512,512]{1,0:T(8,128)(2,1)S(1)} %bitcast.35), channel_id=1, source_target_pairs={{0,1},{1,0},{2,3},{3,2},{4,5},{5,4},{6,7},{7,6},{8,9},{9,8},{10,11... | collective-permute-start | bytes 1572872 | tf_op jit(solution)/shard_map/ppermute | solution.py:174
  29.1 41.1 %collective-permute-start.2 = (bf16[2,64,512]{2,1,0:T(8,128)(2,1)S(1)}, bf16[2,64,512]{2,1,0:T(8,128)(2,1)}, u32[]{:S(2)}, u32[]{:S(2)}) collective-permute-start(bf16[2,64,512]{2,1,0:T(8,128)(2,1)S(1)} %fusion.10), channel_id=1, source_target_pairs={{0,384},{384,0},{1,385},{385,1},{2,386},{386,2},{3,387},{387,3},{4... | collective-permute-start | bytes 393224 | tf_op jit(solution)/shard_map/ppermute | solution.py:27
  65.0 69.9 %all-to-all-start.1 = ((bf16[8,128,512]{2,1,0:T(8,128)(2,1)}), bf16[8,128,512]{2,1,0:T(8,128)(2,1)S(1)}, u32[]{:S(2)}, u32[]{:S(2)}) async-start(bf16[8,128,512]{2,1,0:T(8,128)(2,1)} %partial_keys.1), calls=%async_computation.1 | async-start | bytes 2097152 | tf_op jit(solution)/shard_map/all_to_all | solution.py:178
  71.2 9.9 %collective-permute-start.3 = (bf16[64,512]{1,0:T(8,128)(2,1)S(1)}, bf16[64,512]{1,0:T(8,128)(2,1)S(1)}, u32[]{:S(2)}, u32[]{:S(2)}) collective-permute-start(bf16[64,512]{1,0:T(8,128)(2,1)S(1)} %fusion.12), channel_id=1, source_target_pairs={{0,32},{32,0},{1,33},{33,1},{2,34},{34,2},{3,35},{35,3},{4,36},{36... | collective-permute-start | bytes 196616 | tf_op jit(solution)/shard_map/ppermute | solution.py:27
  79.2 47.5 %copy-start.1 = (bf16[1,512,512]{2,1,0:T(8,128)(2,1)S(1)}, bf16[1,512,512]{2,1,0:T(8,128)(2,1)}, u32[]{:S(2)}) copy-start(bf16[1,512,512]{2,1,0:T(8,128)(2,1)} %param.8) | copy-start | bytes 1572868
  79.2 47.5 %copy-start.12 = (f32[512,512]{1,0:T(8,128)S(1)}, f32[512,512]{1,0:T(8,128)}, u32[]{:S(2)}) copy-start(f32[512,512]{1,0:T(8,128)} %param.10) | copy-start | bytes 3145732
  129.9 5.0 %copy-start.10 = (bf16[128,512]{1,0:T(8,128)(2,1)S(1)}, bf16[128,512]{1,0:T(8,128)(2,1)}, u32[]{:S(2)}) copy-start(bf16[128,512]{1,0:T(8,128)(2,1)} %target_ref.1) | copy-start | bytes 393220
  131.7 0.8 copy-start.2
  132.5 0.8 copy-start.4
  133.3 0.8 copy-start.6
  134.1 0.8 copy-start.8
  134.9 24.9 %copy-start.11 = (f32[512,512]{1,0:T(8,128)S(1)}, f32[512,512]{1,0:T(8,128)}, u32[]{:S(2)}) copy-start(f32[512,512]{1,0:T(8,128)} %get-tuple-element.14) | copy-start | bytes 3145732
  134.9 24.9 %copy-start.9 = (bf16[512,512]{1,0:T(8,128)(2,1)S(1)}, bf16[512,512]{1,0:T(8,128)(2,1)}, u32[]{:S(2)}) copy-start(bf16[512,512]{1,0:T(8,128)(2,1)} %copy-done.8) | copy-start | bytes 1572868
  154.3 5.9 %copy-start.7 = (bf16[512,512]{1,0:T(8,128)(2,1)S(1)}, bf16[512,512]{1,0:T(8,128)(2,1)}, u32[]{:S(2)}) copy-start(bf16[512,512]{1,0:T(8,128)(2,1)} %copy-done.6) | copy-start | bytes 1572868
  154.3 8.3 %collective-permute-start.4 = (bf16[512,256]{1,0:T(8,128)(2,1)S(1)}, bf16[512,256]{1,0:T(8,128)(2,1)S(1)}, u32[]{:S(2)}, u32[]{:S(2)}) collective-permute-start(bf16[512,256]{1,0:T(8,128)(2,1)S(1)} %get-tuple-element.25), channel_id=1, source_target_pairs={{0,2},{2,0},{1,3},{3,1},{4,6},{6,4},{5,7},{7,5},{8,10},{10,8},{9,1... | collective-permute-start | bytes 786440 | tf_op jit(solution)/shard_map/ppermute | solution.py:191
  156.4 11.9 %collective-permute-start.6 = (bf16[512,256]{1,0:T(8,128)(2,1)S(1)}, bf16[512,256]{1,0:T(8,128)(2,1)S(1)}, u32[]{:S(2)}, u32[]{:S(2)}) collective-permute-start(bf16[512,256]{1,0:T(8,128)(2,1)S(1)} %get-tuple-element.26), channel_id=1, source_target_pairs={{0,2},{2,0},{1,3},{3,1},{4,6},{6,4},{5,7},{7,5},{8,10},{10,8},{9,1... | collective-permute-start | bytes 786440 | tf_op jit(solution)/shard_map/ppermute | solution.py:191
  159.8 2.8 %copy-start.5 = (bf16[512,512]{1,0:T(8,128)(2,1)S(1)}, bf16[512,512]{1,0:T(8,128)(2,1)}, u32[]{:S(2)}) copy-start(bf16[512,512]{1,0:T(8,128)(2,1)} %copy-done.4) | copy-start | bytes 1572868
  160.7 11.5 %copy-start.3 = (bf16[512,512]{1,0:T(8,128)(2,1)S(1)}, bf16[512,512]{1,0:T(8,128)(2,1)}, u32[]{:S(2)}) copy-start(bf16[512,512]{1,0:T(8,128)(2,1)} %copy-done.2) | copy-start | bytes 1572868
  162.9 9.9 %collective-permute-start.5 = (bf16[512,256]{1,0:T(8,128)(2,1)S(1)}, bf16[512,256]{1,0:T(8,128)(2,1)S(1)}, u32[]{:S(2)}, u32[]{:S(2)}) collective-permute-start(bf16[512,256]{1,0:T(8,128)(2,1)S(1)} %fusion.5), channel_id=1, source_target_pairs={{0,1},{1,0},{2,3},{3,2},{4,5},{5,4},{6,7},{7,6},{8,9},{9,8},{10,11... | collective-permute-start | bytes 786440 | tf_op jit(solution)/shard_map/ppermute | solution.py:203
  168.5 11.2 %collective-permute-start.7 = (bf16[512,256]{1,0:T(8,128)(2,1)S(1)}, bf16[512,256]{1,0:T(8,128)(2,1)S(1)}, u32[]{:S(2)}, u32[]{:S(2)}) collective-permute-start(bf16[512,256]{1,0:T(8,128)(2,1)S(1)} %fusion.6), channel_id=1, source_target_pairs={{0,1},{1,0},{2,3},{3,2},{4,5},{5,4},{6,7},{7,6},{8,9},{9,8},{10,11... | collective-permute-start | bytes 786440 | tf_op jit(solution)/shard_map/ppermute | solution.py:203

commit v2 on v1

--- a/solution.py
+++ b/solution.py
@@ -11,7 +11,7 @@
 
 Y = ("yh", "yl")
 FSDP = ("yh", "yl", "xh")
-REPLICA = ("xl", "zh", "zl", "core")
+REPLICA = ("xl", "z2", "z1", "z0", "core")
 SWAP = [(0, 1), (1, 0)]
 VMEM_LIMIT = 16 * 2**20
 
@@ -24,7 +24,7 @@
 def halved(total, axis, dim):
     me = lax.axis_index(axis)
     sent = lax.dynamic_index_in_dim(total, 1 - me, dim, keepdims=False).astype(jnp.bfloat16)
-    got = lax.ppermute(sent, axis, SWAP)
+    got = lax.dynamic_index_in_dim(lax.all_gather(sent, axis), 1 - me, 0, keepdims=False)
     return lax.dynamic_index_in_dim(total, me, dim, keepdims=False) + got.astype(jnp.float32)
 
 
@@ -34,37 +34,67 @@
     total = pseudo.reshape(2, 2, 2, rows // 8, columns)
     total = halved(total, "core", 2)
     total = halved(total, "xl", 0)
-    total = halved(total, "zl", 0)
-    parts = lax.all_gather(total.astype(jnp.bfloat16), "zh", axis=0)
-    mean = (jnp.sum(parts.astype(jnp.float32), axis=0) / replicas).astype(jnp.bfloat16)
-    return lax.all_gather(mean, ("xl", "zl", "core"), axis=0, tiled=True).astype(jnp.float32)
-
-
-def split_kernel(tokens_ref, out_ref):
-    out_ref[0] = tokens_ref[...]
+    total = halved(total, "z0", 0)
+    own = total.astype(jnp.bfloat16)
+    other = lax.ppermute(own, "z1", SWAP)
+    own = (own.astype(jnp.float32) + other.astype(jnp.float32)).astype(jnp.bfloat16)
+    back1 = lax.ppermute(own, "z2", [(0, 1), (1, 2), (2, 0)])
+    back2 = lax.ppermute(own, "z2", [(0, 2), (1, 0), (2, 1)])
+    me = lax.axis_index("z2")
+
+    def chosen(*values):
+        return jnp.where(me == 0, values[0], jnp.where(me == 1, values[1], values[2])).astype(jnp.float32)
+
+    summed = chosen(own, back1, back2) + chosen(back2, own, back1) + chosen(back1, back2, own)
+    mean = (summed / replicas).astype(jnp.bfloat16)
+    return lax.all_gather(mean, ("xl", "z0", "core"), axis=0, tiled=True).astype(jnp.float32)
+
+
+def split_kernel(tokens_ref, out_ref, held, read, wrote):
+    parts, _, width = held.shape
+
+    def reading(i):
+        return pltpu.make_async_copy(tokens_ref.at[:, i * width : (i + 1) * width], held.at[i], read.at[i])
+
+    def writing(i):
+        return pltpu.make_async_copy(held.at[i], out_ref.at[i], wrote.at[i])
+
+    for i in range(parts):
+        reading(i).start()
+    for i in range(parts):
+        reading(i).wait()
+        writing(i).start()
+    for i in range(parts):
+        writing(i).wait()
 
 
 def split_columns(tokens, parts):
     rows, columns = tokens.shape
-    width = columns // parts
+    shape = (parts, rows, columns // parts)
     return pl.pallas_call(
         split_kernel,
-        grid=(parts,),
-        in_specs=[pl.BlockSpec((rows, width), lambda i: (0, i))],
-        out_specs=pl.BlockSpec((1, rows, width), lambda i: (i, 0, 0)),
-        out_shape=jax.ShapeDtypeStruct((parts, rows, width), tokens.dtype),
+        in_specs=[pl.BlockSpec(memory_space=pl.ANY)],
+        out_specs=pl.BlockSpec(memory_space=pl.ANY),
+        out_shape=jax.ShapeDtypeStruct(shape, tokens.dtype),
+        scratch_shapes=[
+            pltpu.VMEM(shape, tokens.dtype),
+            pltpu.SemaphoreType.DMA((parts,)),
+            pltpu.SemaphoreType.DMA((parts,)),
+        ],
         name="split_columns",
     )(tokens)
 
 
 def partial_kernel(scale, place_ref, x_ref, own_ref, other_ref, out_ref):
     width = own_ref.shape[0]
-    low, high = x_ref[0, :, :width], x_ref[0, :, width:]
+    rows = x_ref.shape[0] * x_ref.shape[1]
+    low = x_ref[:, :, :width].reshape(rows, width)
+    high = x_ref[:, :, width:].reshape(rows, width)
 
     def emit(low_rows, high_rows):
         total = jnp.dot(low, low_rows[...], preferred_element_type=jnp.float32)
         total += jnp.dot(high, high_rows[...], preferred_element_type=jnp.float32)
-        out_ref[0] = (total * scale).astype(out_ref.dtype)
+        out_ref[...] = (total * scale).astype(out_ref.dtype).reshape(out_ref.shape)
 
     @pl.when(place_ref[1] == 0)
     def _():
@@ -83,9 +113,9 @@
         functools.partial(partial_kernel, scale),
         grid_spec=pltpu.PrefetchScalarGridSpec(
             num_scalar_prefetch=1,
-            grid=(parts,),
-            in_specs=[pl.BlockSpec((1, rows, columns), lambda i, place: (i, 0, 0)), whole, whole],
-            out_specs=pl.BlockSpec((1, rows, key_width), lambda i, place: (i, 0, 0)),
+            grid=(2,),
+            in_specs=[pl.BlockSpec((parts // 2, rows, columns), lambda i, place: (i, 0, 0)), whole, whole],
+            out_specs=pl.BlockSpec((parts // 2, rows, key_width), lambda i, place: (i, 0, 0)),
         ),
         out_shape=jax.ShapeDtypeStruct((parts, rows, key_width), jnp.bfloat16),
         cost_estimate=pl.CostEstimate(
@@ -132,7 +162,7 @@
         ),
         out_shape=[out] * 4,
         cost_estimate=pl.CostEstimate(flops=0, bytes_accessed=4 * parts * rows * columns, transcendentals=0),
-        compiler_params=pltpu.CompilerParams(vmem_limit_bytes=VMEM_LIMIT),
+        compiler_params=pltpu.CompilerParams(vmem_limit_bytes=56 * 2**20),
         name="turn",
     )(place, blocks, blocks)
 
@@ -178,11 +208,6 @@
     pieces = lax.all_to_all(partial, Y, 0, 0, tiled=True)
 
     send_near, keep_near, send_far, keep_far = turned(place, blocks)
-    new_momentum = nesterov_coef * momentum + averaged
-    new_global = global_frag - outer_rate * (averaged + nesterov_coef * new_momentum)
-    merged = merge_share * weight_rows.astype(jnp.float32) + (1.0 - merge_share) * new_global
-    new_momentum, new_global, merged = lax.optimization_barrier((new_momentum, new_global, merged))
-
     residual = residual_of(pieces, target)
     near = lax.all_gather(residual, "yh", axis=0, tiled=True)
     cut = key_width // 2
@@ -194,21 +219,28 @@
         return jnp.dot(block, values, preferred_element_type=jnp.float32)
 
     sent_near = product(send_near, near)
-    kept_near = merged - (merge_share * inner_rate * key_scale) * product(keep_near, near)
-    sent_near, kept_near = lax.optimization_barrier((sent_near, kept_near))
+    kept_near = product(keep_near, near)
+    got = []
+    for c in range(2):
+        part = slice(c * cut, (c + 1) * cut)
+        sent = ((sent_near[:, part] + product(send_far, far[c])) * key_scale).astype(jnp.bfloat16)
+        got.append(lax.ppermute(sent, "xh", SWAP))
+
+    averaged, _ = lax.optimization_barrier((averaged, sent))
+    new_momentum = nesterov_coef * momentum + averaged
+    new_global = global_frag - outer_rate * (averaged + nesterov_coef * new_momentum)
+    merged = merge_share * weight_rows.astype(jnp.float32) + (1.0 - merge_share) * new_global
     new_weight = []
     for c in range(2):
         part = slice(c * cut, (c + 1) * cut)
-        sent = ((sent_near[:, part] + product(send_far, far[c])) * key_scale).astype(jnp.bfloat16)
-        got = lax.ppermute(sent, "xh", SWAP)
-        kept = kept_near[:, part] - (merge_share * inner_rate * key_scale) * product(keep_far, far[c])
-        kept = lax.optimization_barrier(kept)
-        new_weight.append((kept - (merge_share * inner_rate) * got.astype(jnp.float32)).astype(jnp.bfloat16))
+        gradient = (kept_near[:, part] + product(keep_far, far[c])) * key_scale
+        kept = lax.optimization_barrier(merged[:, part] - (merge_share * inner_rate) * gradient)
+        new_weight.append((kept - (merge_share * inner_rate) * got[c].astype(jnp.float32)).astype(jnp.bfloat16))
     return (jnp.concatenate(new_weight, axis=1)[None], residual, new_global, new_momentum)
 
 
 def solution(mesh):
-    split = Mesh(mesh.devices.reshape(2, 6, 2, 2, 4, 2, 2), REPLICA + FSDP)
+    split = Mesh(mesh.devices.reshape(2, 3, 2, 2, 2, 4, 2, 2), REPLICA + FSDP)
     rows = P(REPLICA + FSDP, None)
     per_replica = P(REPLICA, FSDP, None)
     shared = P(FSDP, None)

time: 183 us -> 185 us (1.011)
  waiting for transfers between devices: 41.6 us -> 58 us
  blocking collectives: 63.4 us -> 52.5 us
  starting transfers between devices: 45.7 us -> 51.8 us
  local copies, waits for them, and re-layouts: 6 us -> 1.2 us
  other arithmetic: 7.38 us -> 4.21 us
    all_to_all x1, waiting for transfers between devices: 19.2 us -> 33.7 us  [shards(): lax.all_to_all(split_columns(tokens, lax.axis_size(Y)), Y, 0, 0, tiled=True)]
    all_gather x2 -> x4, blocking collectives: 45.5 us -> 34.5 us  [the longest x1 18.2 us: replica_mean(): lax.all_gather(mean, ('xl', 'z0', 'core'), axis=0, tiled=True)]
    ppermute x5, waiting for transfers between devices: 8.77 us -> 13.6 us  [the longest x1 7.13 us: replica_mean(): back1 = lax.ppermute(own, 'z2', [(0, 1), (1, 2), (2, 0)])]
    ppermute x5, starting transfers between devices: 25.5 us -> 29 us  [the longest x1 12.4 us: replica_mean(): back2 = lax.ppermute(own, 'z2', [(0, 2), (1, 0), (2, 1)])]
    pallas_call x1, Pallas kernels: 1.77 us -> 4.96 us  [turned(): pl.pallas_call(turn_kernel, grid_spec=pltpu.PrefetchScalarGridSpec(num_sc...]
    pallas_call x1, Pallas kernels: 5.62 us -> 2.44 us  [split_columns(): pl.pallas_call(split_kernel, in_specs=[pl.BlockSpec(memory_space=pl.ANY)]...]
    unnamed x26 -> x20, local copies, waits for them, and re-layouts: 3.2 us -> 0.05 us
    ppermute x1, starting transfers between devices: 1.92 us -> 4.65 us  [shards(): other_rows = lax.ppermute(weight_rows, 'xh', SWAP)]
  transfers between devices with their start and end apart: 10 -> 10, of which waited for: 6 -> 7; matrix products, arithmetic and copies ran while one was open for 6% -> 3% of each run, Pallas kernels for 4% -> 3%
where the time goes in v2:
time: 185 us; the launch traced here: 183 us
  waiting for transfers between devices  58 us (31%)
  blocking collectives  52.5 us (28%)
  starting transfers between devices  51.8 us (28%)
  Pallas kernels  11.8 us (6%)
  other arithmetic  4.21 us (2%)
  matrix products  2.06 us (1%)
    all_to_all x1, waiting for transfers between devices, shards(): lax.all_to_all(split_columns(tokens, lax.axis_size(Y)), Y, 0, 0, tiled=True)  33.7 us
    all_gather x1, blocking collectives, replica_mean(): lax.all_gather(mean, ('xl', 'z0', 'core'), axis=0, tiled=True)  18.2 us
    all_gather x1, blocking collectives, shards(): near = lax.all_gather(residual, 'yh', axis=0, tiled=True)  18.1 us
    all_gather x3, blocking collectives, halved(): lax.all_gather(sent, axis)  16.3 us
    ppermute x1, starting transfers between devices, replica_mean(): back2 = lax.ppermute(own, 'z2', [(0, 2), (1, 0), (2, 1)])  12.4 us
    ppermute x2, starting transfers between devices, shards(): got.append(lax.ppermute(sent, 'xh', SWAP))  8.85 us
    all_to_all x1, starting transfers between devices, shards(): lax.all_to_all(split_columns(tokens, lax.axis_size(Y)), Y, 0, 0, tiled=True)  7.78 us
    ppermute x1, waiting for transfers between devices, shards(): other_rows = lax.ppermute(weight_rows, 'xh', SWAP)  7.74 us
  transfers between devices with their start and end apart: 10, of which 7 were waited for; matrix products, arithmetic and copies ran while one was open for 3% of the time, Pallas kernels for 3%

profile of v2, /device:TPU:1, one launch (start us, length us, event | category | flops | bytes accessed | tf_op | source)
XLA Modules:
  0.0 182.6 jit_solution(17626271930328892195)
XLA Ops:
  0.6 2.4 %split_columns.1 = bf16[8,128,1024]{2,1,0:T(8,128)(2,1)} custom-call(bf16[128,8192]{1,0:T(8,128)(2,1)} %tokens_ref.1), custom_call_target="tpu_custom_call" | custom-call | tf_op jit(solution)/shard_map/split_columns/pallas_call | solution.py:74
  3.1 7.8 %all-to-all-start = ((bf16[8,128,1024]{2,1,0:T(8,128)(2,1)}), bf16[8,128,1024]{2,1,0:T(8,128)(2,1)S(1)}, u32[]{:S(2)}, u32[]{:S(2)}) async-start(bf16[8,128,1024]{2,1,0:T(8,128)(2,1)} %split_columns.1), calls=%async_computation | async-start | bytes 4194304 | tf_op jit(solution)/shard_map/all_to_all | solution.py:202
  10.9 4.7 %collective-permute-start.3 = (bf16[512,512]{1,0:T(8,128)(2,1)S(1)}, bf16[512,512]{1,0:T(8,128)(2,1)S(1)}, u32[]{:S(2)}, u32[]{:S(2)}) collective-permute-start(bf16[512,512]{1,0:T(8,128)(2,1)S(1)} %bitcast.27), channel_id=1, source_target_pairs={{0,1},{1,0},{2,3},{3,2},{4,5},{5,4},{6,7},{7,6},{8,9},{9,8},{10,11... | collective-permute-start | bytes 1572872 | tf_op jit(solution)/shard_map/ppermute | solution.py:204
  15.6 7.7 %collective-permute-done.3.other_ref = bf16[512,512]{1,0:T(8,128)(2,1)S(1)} collective-permute-done((bf16[512,512]{1,0:T(8,128)(2,1)S(1)}, bf16[512,512]{1,0:T(8,128)(2,1)S(1)}, u32[]{:S(2)}, u32[]{:S(2)}) %collective-permute-start.3) | collective-permute-done | bytes 524320 | tf_op jit(solution)/shard_map/ppermute | solution.py:204
  23.4 33.7 %all-to-all-done.near_ref.far_ref.x_ref = bf16[8,128,1024]{2,1,0:T(8,128)(2,1)S(1)} async-done(((bf16[8,128,1024]{2,1,0:T(8,128)(2,1)}), bf16[8,128,1024]{2,1,0:T(8,128)(2,1)S(1)}, u32[]{:S(2)}, u32[]{:S(2)}) %all-to-all-start) | async-done | bytes 2097184 | tf_op jit(solution)/shard_map/all_to_all | solution.py:202
  57.1 2.9 %partial_keys.1 = bf16[8,128,512]{2,1,0:T(8,128)(2,1)} custom-call(s32[2]{0:T(128)S(1)} %pad_add_fusion.place_ref, bf16[8,128,1024]{2,1,0:T(8,128)(2,1)S(1)} %all-to-all-done.near_ref.far_ref.x_ref, bf16[512,512]{1,0:T(8,128)(2,1)S(1)} %bitcast.28, bf16[512,512]{1,0:T(8,128)(2,1)S(1)} %collective-permute-done.3.other_ref), custom_call_target="tpu_custom_call" | custom-call | flops 1073741824 | bytes 4194304 | tf_op jit(solution)/shard_map/partial_keys/pallas_call | solution.py:112
  60.0 5.1 %all-to-all-start.1 = ((bf16[8,128,512]{2,1,0:T(8,128)(2,1)}), bf16[8,128,512]{2,1,0:T(8,128)(2,1)S(1)}, u32[]{:S(2)}, u32[]{:S(2)}) async-start(bf16[8,128,512]{2,1,0:T(8,128)(2,1)} %partial_keys.1), calls=%async_computation.1 | async-start | bytes 2097152 | tf_op jit(solution)/shard_map/all_to_all | solution.py:208
  65.1 1.1 dynamic-slice_convert_fusion
  66.2 6.3 %all-gather = bf16[4,2,1,64,512]{4,3,2,1,0:T(8,128)(2,1)S(1)} all-gather(bf16[2,2,1,64,512]{4,3,2,1,0:T(8,128)(2,1)S(1)} %dynamic-slice_convert_fusion), channel_id=2, replica_groups=mesh['xl'=2,'z2'=3,'z1'=2,'z0'=2,'core'=2,'yh'=4,'yl'=2,'xh'=2] {'core'}, dimensions={0}, use_global_device_ids=true | all-gather | bytes 786432 | tf_op jit(solution)/shard_map/all_gather | solution.py:27
  72.5 1.1 convert_add_fusion
  73.6 5.3 %all_gather.19 = bf16[2,2,64,512]{3,2,1,0:T(8,128)(2,1)S(1)} all-gather(bf16[1,2,64,512]{3,2,1,0:T(8,128)(2,1)S(1)} %dynamic-slice_convert_fusion.1), channel_id=1, replica_groups=mesh['xl'=2,'z2'=3,'z1'=2,'z0'=2,'core'=2,'yh'=4,'yl'=2,'xh'=2] {'xl'}, dimensions={0}, use_global_device_ids=true | all-gather | bytes 393216 | tf_op jit(solution)/shard_map/all_gather | solution.py:27
  79.0 4.6 %all-gather.1 = bf16[2,1,64,512]{3,2,1,0:T(8,128)(2,1)S(1)} all-gather(bf16[1,1,64,512]{3,2,1,0:T(8,128)(2,1)S(1)} %dynamic-slice_convert_fusion.2), channel_id=3, replica_groups=mesh['xl'=2,'z2'=3,'z1'=2,'z0'=2,'core'=2,'yh'=4,'yl'=2,'xh'=2] {'z0'}, dimensions={0}, use_global_device_ids=true | all-gather | bytes 196608 | tf_op jit(solution)/shard_map/all_gather | solution.py:27
  83.7 5.8 %collective-permute-start = (bf16[64,512]{1,0:T(8,128)(2,1)S(1)}, bf16[64,512]{1,0:T(8,128)(2,1)S(1)}, u32[]{:S(2)}, u32[]{:S(2)}) collective-permute-start(bf16[64,512]{1,0:T(8,128)(2,1)S(1)} %fusion.8), channel_id=1, source_target_pairs={{0,64},{64,0},{1,65},{65,1},{2,66},{66,2},{3,67},{67,3},{4,68},{68... | collective-permute-start | bytes 196616 | tf_op jit(solution)/shard_map/ppermute | solution.py:39
  89.5 1.6 collective-permute-done
  91.2 12.4 %collective-permute-start.2 = (bf16[64,512]{1,0:T(8,128)(2,1)S(1)}, bf16[64,512]{1,0:T(8,128)(2,1)S(1)}, u32[]{:S(2)}, u32[]{:S(2)}) collective-permute-start(bf16[64,512]{1,0:T(8,128)(2,1)S(1)} %add_convert_fusion.1), channel_id=1, source_target_pairs={{0,256},{128,0},{256,128},{1,257},{129,1},{257,129},{2,258},{130,2... | collective-permute-start | bytes 196616 | tf_op jit(solution)/shard_map/ppermute | solution.py:42
  103.6 1.9 %collective-permute-start.1 = (bf16[64,512]{1,0:T(8,128)(2,1)S(1)}, bf16[64,512]{1,0:T(8,128)(2,1)S(1)}, u32[]{:S(2)}, u32[]{:S(2)}) collective-permute-start(bf16[64,512]{1,0:T(8,128)(2,1)S(1)} %add_convert_fusion.1), channel_id=1, source_target_pairs={{0,128},{128,256},{256,0},{1,129},{129,257},{257,1},{2,130},{130,2... | collective-permute-start | bytes 196616 | tf_op jit(solution)/shard_map/ppermute | solution.py:41
  105.6 7.1 %collective-permute-done.1 = bf16[64,512]{1,0:T(8,128)(2,1)S(1)} collective-permute-done((bf16[64,512]{1,0:T(8,128)(2,1)S(1)}, bf16[64,512]{1,0:T(8,128)(2,1)S(1)}, u32[]{:S(2)}, u32[]{:S(2)}) %collective-permute-start.1) | collective-permute-done | bytes 65568 | tf_op jit(solution)/shard_map/ppermute | solution.py:41
  112.8 18.2 %all_gather.21 = bf16[512,512]{1,0:T(8,128)(2,1)S(1)} all-gather(bf16[64,512]{1,0:T(8,128)(2,1)S(1)} %multiply_convert_fusion), channel_id=1, replica_groups=mesh['xl'=2,'z2'=3,'z1'=2,'z0'=2,'core'=2,'yh'=4,'yl'=2,'xh'=2] {'xl','z..., dimensions={0}, use_global_device_ids=true | all-gather | bytes 589824 | tf_op jit(solution)/shard_map/all_gather | solution.py:50
  131.1 5.0 %turn.1 = (bf16[512,512]{1,0:T(8,128)(2,1)}, bf16[512,512]{1,0:T(8,128)(2,1)}, bf16[512,512]{1,0:T(8,128)(2,1)}, bf16[512,512]{1,0:T(8,128)(2,1)}) custom-call(s32[2]{0:T(128)} %copy-done.3, bf16[8,128,1024]{2,1,0:T(8,128)(2,1)} %copy-done, bf16[8,128,1024]{2,1,0:T(8,128)(2,1)} %copy-done), custom_call_target="tpu_custom_call" | custom-call | bytes 4194304 | tf_op jit(solution)/shard_map/turn/pallas_call | solution.py:152
  136.0 1.5 residual.1
  137.5 18.1 %all_gather.22 = bf16[512,512]{1,0:T(8,128)(2,1)S(1)} all-gather(bf16[128,512]{1,0:T(8,128)(2,1)} %residual.1), channel_id=1, replica_groups=mesh['xl'=2,'z2'=3,'z1'=2,'z0'=2,'core'=2,'yh'=4,'yl'=2,'xh'=2] {'yh'}, dimensions={0}, use_global_device_ids=true | all-gather | bytes 655360 | tf_op jit(solution)/shard_map/all_gather | solution.py:212
  155.6 0.4 fusion.11
  156.1 1.9 %collective-permute-start.5 = (bf16[512,256]{1,0:T(8,128)(2,1)S(1)}, bf16[512,256]{1,0:T(8,128)(2,1)S(1)}, u32[]{:S(2)}, u32[]{:S(2)}) collective-permute-start(bf16[512,256]{1,0:T(8,128)(2,1)S(1)} %get-tuple-element.17), channel_id=1, source_target_pairs={{0,2},{2,0},{1,3},{3,1},{4,6},{6,4},{5,7},{7,5},{8,10},{10,8},{9,1... | collective-permute-start | bytes 786440 | tf_op jit(solution)/shard_map/ppermute | solution.py:216
  158.0 3.4 %collective-permute-start.4 = (bf16[512,256]{1,0:T(8,128)(2,1)S(1)}, bf16[512,256]{1,0:T(8,128)(2,1)S(1)}, u32[]{:S(2)}, u32[]{:S(2)}) collective-permute-start(bf16[512,256]{1,0:T(8,128)(2,1)S(1)} %get-tuple-element.18), channel_id=1, source_target_pairs={{0,2},{2,0},{1,3},{3,1},{4,6},{6,4},{5,7},{7,5},{8,10},{10,8},{9,1... | collective-permute-start | bytes 786440 | tf_op jit(solution)/shard_map/ppermute | solution.py:216
  161.4 0.4 fusion.10
  161.8 2.0 %collective-permute-done.5 = bf16[512,256]{1,0:T(8,128)(2,1)S(1)} collective-permute-done((bf16[512,256]{1,0:T(8,128)(2,1)S(1)}, bf16[512,256]{1,0:T(8,128)(2,1)S(1)}, u32[]{:S(2)}, u32[]{:S(2)}) %collective-permute-start.5) | collective-permute-done | bytes 262176 | tf_op jit(solution)/shard_map/ppermute | solution.py:216
  164.2 4.4 %collective-permute-start.6 = (bf16[512,256]{1,0:T(8,128)(2,1)S(1)}, bf16[512,256]{1,0:T(8,128)(2,1)S(1)}, u32[]{:S(2)}, u32[]{:S(2)}) collective-permute-start(bf16[512,256]{1,0:T(8,128)(2,1)S(1)} %fusion.7), channel_id=1, source_target_pairs={{0,1},{1,0},{2,3},{3,2},{4,5},{5,4},{6,7},{7,6},{8,9},{9,8},{10,11... | collective-permute-start | bytes 786440 | tf_op jit(solution)/shard_map/ppermute | solution.py:227
  168.6 0.9 collective-permute-done.4
  169.8 4.5 %collective-permute-start.7 = (bf16[512,256]{1,0:T(8,128)(2,1)S(1)}, bf16[512,256]{1,0:T(8,128)(2,1)S(1)}, u32[]{:S(2)}, u32[]{:S(2)}) collective-permute-start(bf16[512,256]{1,0:T(8,128)(2,1)S(1)} %fusion.6), channel_id=1, source_target_pairs={{0,1},{1,0},{2,3},{3,2},{4,5},{5,4},{6,7},{7,6},{8,9},{9,8},{10,11... | collective-permute-start | bytes 786440 | tf_op jit(solution)/shard_map/ppermute | solution.py:227
  174.3 1.8 add_multiply_fusion
  176.8 4.8 %collective-permute-done.7 = bf16[512,256]{1,0:T(8,128)(2,1)S(1)} collective-permute-done((bf16[512,256]{1,0:T(8,128)(2,1)S(1)}, bf16[512,256]{1,0:T(8,128)(2,1)S(1)}, u32[]{:S(2)}, u32[]{:S(2)}) %collective-permute-start.7) | collective-permute-done | bytes 262176 | tf_op jit(solution)/shard_map/ppermute | solution.py:227
  181.7 0.8 maximum_bitcast_fusion
  (38 shorter events, 1.8 us)
Async XLA Ops:
  3.1 7.8 %copy-start.1 = (bf16[1,512,512]{2,1,0:T(8,128)(2,1)S(1)}, bf16[1,512,512]{2,1,0:T(8,128)(2,1)}, u32[]{:S(2)}) copy-start(bf16[1,512,512]{2,1,0:T(8,128)(2,1)} %param.8) | copy-start | bytes 1572868
  3.1 54.0 %all-to-all-start = ((bf16[8,128,1024]{2,1,0:T(8,128)(2,1)}), bf16[8,128,1024]{2,1,0:T(8,128)(2,1)S(1)}, u32[]{:S(2)}, u32[]{:S(2)}) async-start(bf16[8,128,1024]{2,1,0:T(8,128)(2,1)} %split_columns.1), calls=%async_computation | async-start | bytes 4194304 | tf_op jit(solution)/shard_map/all_to_all | solution.py:202
  10.9 12.5 %collective-permute-start.3 = (bf16[512,512]{1,0:T(8,128)(2,1)S(1)}, bf16[512,512]{1,0:T(8,128)(2,1)S(1)}, u32[]{:S(2)}, u32[]{:S(2)}) collective-permute-start(bf16[512,512]{1,0:T(8,128)(2,1)S(1)} %bitcast.27), channel_id=1, source_target_pairs={{0,1},{1,0},{2,3},{3,2},{4,5},{5,4},{6,7},{7,6},{8,9},{9,8},{10,11... | collective-permute-start | bytes 1572872 | tf_op jit(solution)/shard_map/ppermute | solution.py:204
  15.6 44.4 %copy-start.3 = (s32[2]{0:T(128)}, s32[2]{0:T(128)S(1)}, u32[]{:S(2)}) copy-start(s32[2]{0:T(128)S(1)} %pad_add_fusion.place_ref) | copy-start | bytes 28
  57.1 2.9 %copy-start = (bf16[8,128,1024]{2,1,0:T(8,128)(2,1)}, bf16[8,128,1024]{2,1,0:T(8,128)(2,1)S(1)}, u32[]{:S(2)}) copy-start(bf16[8,128,1024]{2,1,0:T(8,128)(2,1)S(1)} %all-to-all-done.near_ref.far_ref.x_ref) | copy-start | bytes 6291460
  60.0 76.0 %all-to-all-start.1 = ((bf16[8,128,512]{2,1,0:T(8,128)(2,1)}), bf16[8,128,512]{2,1,0:T(8,128)(2,1)S(1)}, u32[]{:S(2)}, u32[]{:S(2)}) async-start(bf16[8,128,512]{2,1,0:T(8,128)(2,1)} %partial_keys.1), calls=%async_computation.1 | async-start | bytes 2097152 | tf_op jit(solution)/shard_map/all_to_all | solution.py:208
  83.7 7.5 %collective-permute-start = (bf16[64,512]{1,0:T(8,128)(2,1)S(1)}, bf16[64,512]{1,0:T(8,128)(2,1)S(1)}, u32[]{:S(2)}, u32[]{:S(2)}) collective-permute-start(bf16[64,512]{1,0:T(8,128)(2,1)S(1)} %fusion.8), channel_id=1, source_target_pairs={{0,64},{64,0},{1,65},{65,1},{2,66},{66,2},{3,67},{67,3},{4,68},{68... | collective-permute-start | bytes 196616 | tf_op jit(solution)/shard_map/ppermute | solution.py:39
  91.2 14.4 %collective-permute-start.2 = (bf16[64,512]{1,0:T(8,128)(2,1)S(1)}, bf16[64,512]{1,0:T(8,128)(2,1)S(1)}, u32[]{:S(2)}, u32[]{:S(2)}) collective-permute-start(bf16[64,512]{1,0:T(8,128)(2,1)S(1)} %add_convert_fusion.1), channel_id=1, source_target_pairs={{0,256},{128,0},{256,128},{1,257},{129,1},{257,129},{2,258},{130,2... | collective-permute-start | bytes 196616 | tf_op jit(solution)/shard_map/ppermute | solution.py:42
  103.6 9.1 %collective-permute-start.1 = (bf16[64,512]{1,0:T(8,128)(2,1)S(1)}, bf16[64,512]{1,0:T(8,128)(2,1)S(1)}, u32[]{:S(2)}, u32[]{:S(2)}) collective-permute-start(bf16[64,512]{1,0:T(8,128)(2,1)S(1)} %add_convert_fusion.1), channel_id=1, source_target_pairs={{0,128},{128,256},{256,0},{1,129},{129,257},{257,1},{2,130},{130,2... | collective-permute-start | bytes 196616 | tf_op jit(solution)/shard_map/ppermute | solution.py:41
  131.0 5.0 %copy-start.2 = (bf16[128,512]{1,0:T(8,128)(2,1)S(1)}, bf16[128,512]{1,0:T(8,128)(2,1)}, u32[]{:S(2)}) copy-start(bf16[128,512]{1,0:T(8,128)(2,1)} %target_ref.1) | copy-start | bytes 393220
  136.0 19.6 %copy-start.9 = (bf16[512,512]{1,0:T(8,128)(2,1)S(1)}, bf16[512,512]{1,0:T(8,128)(2,1)}, u32[]{:S(2)}) copy-start(bf16[512,512]{1,0:T(8,128)(2,1)} %get-tuple-element.12) | copy-start | bytes 1572868
  137.5 23.9 %copy-start.8 = (bf16[512,512]{1,0:T(8,128)(2,1)S(1)}, bf16[512,512]{1,0:T(8,128)(2,1)}, u32[]{:S(2)}) copy-start(bf16[512,512]{1,0:T(8,128)(2,1)} %get-tuple-element.9) | copy-start | bytes 1572868
  155.6 8.3 %copy-start.4 = (bf16[512,512]{1,0:T(8,128)(2,1)S(1)}, bf16[512,512]{1,0:T(8,128)(2,1)}, u32[]{:S(2)}) copy-start(bf16[512,512]{1,0:T(8,128)(2,1)} %get-tuple-element.10) | copy-start | bytes 1572868
  156.1 7.8 %collective-permute-start.5 = (bf16[512,256]{1,0:T(8,128)(2,1)S(1)}, bf16[512,256]{1,0:T(8,128)(2,1)S(1)}, u32[]{:S(2)}, u32[]{:S(2)}) collective-permute-start(bf16[512,256]{1,0:T(8,128)(2,1)S(1)} %get-tuple-element.17), channel_id=1, source_target_pairs={{0,2},{2,0},{1,3},{3,1},{4,6},{6,4},{5,7},{7,5},{8,10},{10,8},{9,1... | collective-permute-start | bytes 786440 | tf_op jit(solution)/shard_map/ppermute | solution.py:216
  158.0 11.5 %collective-permute-start.4 = (bf16[512,256]{1,0:T(8,128)(2,1)S(1)}, bf16[512,256]{1,0:T(8,128)(2,1)S(1)}, u32[]{:S(2)}, u32[]{:S(2)}) collective-permute-start(bf16[512,256]{1,0:T(8,128)(2,1)S(1)} %get-tuple-element.18), channel_id=1, source_target_pairs={{0,2},{2,0},{1,3},{3,1},{4,6},{6,4},{5,7},{7,5},{8,10},{10,8},{9,1... | collective-permute-start | bytes 786440 | tf_op jit(solution)/shard_map/ppermute | solution.py:216
  161.8 12.5 %copy-start.6 = (f32[512,512]{1,0:T(8,128)S(1)}, f32[512,512]{1,0:T(8,128)}, u32[]{:S(2)}) copy-start(f32[512,512]{1,0:T(8,128)} %param.10) | copy-start | bytes 3145732
  161.8 12.5 %copy-start.7 = (f32[512,512]{1,0:T(8,128)S(1)}, f32[512,512]{1,0:T(8,128)}, u32[]{:S(2)}) copy-start(f32[512,512]{1,0:T(8,128)} %param.11) | copy-start | bytes 3145732
  164.2 12.5 %collective-permute-start.6 = (bf16[512,256]{1,0:T(8,128)(2,1)S(1)}, bf16[512,256]{1,0:T(8,128)(2,1)S(1)}, u32[]{:S(2)}, u32[]{:S(2)}) collective-permute-start(bf16[512,256]{1,0:T(8,128)(2,1)S(1)} %fusion.7), channel_id=1, source_target_pairs={{0,1},{1,0},{2,3},{3,2},{4,5},{5,4},{6,7},{7,6},{8,9},{9,8},{10,11... | collective-permute-start | bytes 786440 | tf_op jit(solution)/shard_map/ppermute | solution.py:227
  169.8 6.3 %copy-start.5 = (bf16[512,512]{1,0:T(8,128)(2,1)S(1)}, bf16[512,512]{1,0:T(8,128)(2,1)}, u32[]{:S(2)}) copy-start(bf16[512,512]{1,0:T(8,128)(2,1)} %get-tuple-element.13) | copy-start | bytes 1572868
  169.8 11.9 %collective-permute-start.7 = (bf16[512,256]{1,0:T(8,128)(2,1)S(1)}, bf16[512,256]{1,0:T(8,128)(2,1)S(1)}, u32[]{:S(2)}, u32[]{:S(2)}) collective-permute-start(bf16[512,256]{1,0:T(8,128)(2,1)S(1)} %fusion.6), channel_id=1, source_target_pairs={{0,1},{1,0},{2,3},{3,2},{4,5},{5,4},{6,7},{7,6},{8,9},{9,8},{10,11... | collective-permute-start | bytes 786440 | tf_op jit(solution)/shard_map/ppermute | solution.py:227

commit v3 on v2

--- a/solution.py
+++ b/solution.py
@@ -9,7 +9,7 @@
 from jax.sharding import PartitionSpec as P
 
 
-Y = ("yh", "yl")
+Y = ("yl", "yh")
 FSDP = ("yh", "yl", "xh")
 REPLICA = ("xl", "z2", "z1", "z0", "core")
 SWAP = [(0, 1), (1, 0)]
@@ -57,7 +57,8 @@
         return pltpu.make_async_copy(tokens_ref.at[:, i * width : (i + 1) * width], held.at[i], read.at[i])
 
     def writing(i):
-        return pltpu.make_async_copy(held.at[i], out_ref.at[i], wrote.at[i])
+        place = i % 2 * (parts // 2) + i // 2
+        return pltpu.make_async_copy(held.at[i], out_ref.at[place], wrote.at[i])
 
     for i in range(parts):
         reading(i).start()
@@ -85,47 +86,34 @@
     )(tokens)
 
 
-def partial_kernel(scale, place_ref, x_ref, own_ref, other_ref, out_ref):
-    width = own_ref.shape[0]
-    rows = x_ref.shape[0] * x_ref.shape[1]
-    low = x_ref[:, :, :width].reshape(rows, width)
-    high = x_ref[:, :, width:].reshape(rows, width)
-
-    def emit(low_rows, high_rows):
-        total = jnp.dot(low, low_rows[...], preferred_element_type=jnp.float32)
-        total += jnp.dot(high, high_rows[...], preferred_element_type=jnp.float32)
-        out_ref[...] = (total * scale).astype(out_ref.dtype).reshape(out_ref.shape)
-
-    @pl.when(place_ref[1] == 0)
-    def _():
-        emit(own_ref, other_ref)
-
-    @pl.when(place_ref[1] != 0)
-    def _():
-        emit(other_ref, own_ref)
-
-
-def partial_keys(place, blocks, own_rows, other_rows, scale):
+def partial_kernel(scale, x_ref, rows_ref, out_ref):
+    parts, rows, columns = x_ref.shape
+    total = jnp.dot(
+        x_ref[...].reshape(parts * rows, columns), rows_ref[...], preferred_element_type=jnp.float32
+    )
+    out_ref[...] = (total * scale).astype(out_ref.dtype).reshape(out_ref.shape)
+
+
+def partial_keys(blocks, weight_rows, scale):
     parts, rows, columns = blocks.shape
-    width, key_width = own_rows.shape
-    whole = pl.BlockSpec((width, key_width), lambda i, place: (0, 0))
+    key_width = weight_rows.shape[1]
     return pl.pallas_call(
         functools.partial(partial_kernel, scale),
-        grid_spec=pltpu.PrefetchScalarGridSpec(
-            num_scalar_prefetch=1,
-            grid=(2,),
-            in_specs=[pl.BlockSpec((parts // 2, rows, columns), lambda i, place: (i, 0, 0)), whole, whole],
-            out_specs=pl.BlockSpec((parts // 2, rows, key_width), lambda i, place: (i, 0, 0)),
-        ),
-        out_shape=jax.ShapeDtypeStruct((parts, rows, key_width), jnp.bfloat16),
+        grid=(2,),
+        in_specs=[
+            pl.BlockSpec((parts // 2, rows, columns), lambda i: (i, 0, 0)),
+            pl.BlockSpec((columns, key_width), lambda i: (0, 0)),
+        ],
+        out_specs=pl.BlockSpec((parts // 2, rows, key_width), lambda i: (i, 0, 0)),
+        out_shape=pltpu.HBM((parts, rows, key_width), jnp.bfloat16),
+        compiler_params=pltpu.CompilerParams(vmem_limit_bytes=VMEM_LIMIT),
         cost_estimate=pl.CostEstimate(
             flops=2 * parts * rows * columns * key_width,
-            bytes_accessed=2 * parts * rows * (columns + key_width) + 4 * width * key_width,
+            bytes_accessed=2 * parts * rows * (columns + key_width) + 2 * columns * key_width,
             transcendentals=0,
         ),
-        compiler_params=pltpu.CompilerParams(vmem_limit_bytes=VMEM_LIMIT),
         name="partial_keys",
-    )(place, blocks, own_rows, other_rows)
+    )(blocks, weight_rows)
 
 
 def turn_kernel(place_ref, near_ref, far_ref, send_near, keep_near, send_far, keep_far):
@@ -148,63 +136,68 @@
 def turned(place, blocks):
     parts, rows, columns = blocks.shape
     width = columns // 2
-    out = jax.ShapeDtypeStruct((width, parts // 2 * rows), blocks.dtype)
+    out = pltpu.HBM((width, parts // 2 * rows), blocks.dtype)
     return pl.pallas_call(
         turn_kernel,
         grid_spec=pltpu.PrefetchScalarGridSpec(
             num_scalar_prefetch=1,
             grid=(parts // 2,),
             in_specs=[
-                pl.BlockSpec((1, rows, columns), lambda k, place: (2 * k + place[0], 0, 0)),
-                pl.BlockSpec((1, rows, columns), lambda k, place: (2 * k + 1 - place[0], 0, 0)),
+                pl.BlockSpec((1, rows, columns), lambda k, place: (4 * place[0] + k, 0, 0)),
+                pl.BlockSpec((1, rows, columns), lambda k, place: (4 - 4 * place[0] + k, 0, 0)),
             ],
             out_specs=[pl.BlockSpec((width, rows), lambda k, place: (0, k))] * 4,
         ),
         out_shape=[out] * 4,
         cost_estimate=pl.CostEstimate(flops=0, bytes_accessed=4 * parts * rows * columns, transcendentals=0),
-        compiler_params=pltpu.CompilerParams(vmem_limit_bytes=56 * 2**20),
+        compiler_params=pltpu.CompilerParams(vmem_limit_bytes=VMEM_LIMIT),
         name="turn",
     )(place, blocks, blocks)
 
 
 def residual_kernel(pieces_ref, target_ref, out_ref):
-    total = pieces_ref[0].astype(jnp.float32)
-    for f in range(1, pieces_ref.shape[0]):
-        total += pieces_ref[f].astype(jnp.float32)
-    out_ref[...] = (total - target_ref[...].astype(jnp.float32)).astype(out_ref.dtype)
+    step = 16
+
+    def rows_of(i, _):
+        rows = pl.ds(pl.multiple_of(i * step, step), step)
+        total = pieces_ref[0, rows, :].astype(jnp.float32)
+        for f in range(1, pieces_ref.shape[0]):
+            total += pieces_ref[f, rows, :].astype(jnp.float32)
+        out_ref[rows, :] = (total - target_ref[rows, :].astype(jnp.float32)).astype(out_ref.dtype)
+        return _
+
+    lax.fori_loop(0, out_ref.shape[0] // step, rows_of, 0, unroll=True)
 
 
 def residual_of(pieces, target):
-    rows, key_width = target.shape
-    parts = pieces.shape[0]
-    step = rows // 4
+    vmem = pl.BlockSpec(memory_space=pltpu.VMEM)
     return pl.pallas_call(
         residual_kernel,
-        grid=(4,),
-        in_specs=[
-            pl.BlockSpec((parts, step, key_width), lambda i: (0, i, 0)),
-            pl.BlockSpec((step, key_width), lambda i: (i, 0)),
-        ],
-        out_specs=pl.BlockSpec((step, key_width), lambda i: (i, 0)),
-        out_shape=jax.ShapeDtypeStruct((rows, key_width), jnp.bfloat16),
+        in_specs=[vmem, vmem],
+        out_specs=vmem,
+        out_shape=jax.ShapeDtypeStruct(target.shape, jnp.bfloat16),
         compiler_params=pltpu.CompilerParams(vmem_limit_bytes=VMEM_LIMIT),
         name="residual",
     )(pieces, target)
 
 
 def shards(tokens, target, weight, pseudo, global_frag, momentum):
-    _, model_width = tokens.shape
+    own_tokens, model_width = tokens.shape
     key_scale = model_width ** (-0.5)
     weight_rows = weight[0]
-    _, key_width = weight_rows.shape
+    width, key_width = weight_rows.shape
     place = jnp.stack([lax.axis_index("yl"), lax.axis_index("xh")]).astype(jnp.int32)
 
     blocks = lax.all_to_all(split_columns(tokens, lax.axis_size(Y)), Y, 0, 0, tiled=True)
 
     other_rows = lax.ppermute(weight_rows, "xh", SWAP)
+    first = lax.axis_index("xh") == 0
+    both_rows = jnp.concatenate(
+        [jnp.where(first, weight_rows, other_rows), jnp.where(first, other_rows, weight_rows)], axis=0
+    )
     averaged = replica_mean(pseudo[0])
 
-    partial = partial_keys(place, blocks, weight_rows, other_rows, key_scale)
+    partial = partial_keys(blocks, both_rows, key_scale)
     pieces = lax.all_to_all(partial, Y, 0, 0, tiled=True)
 
     send_near, keep_near, send_far, keep_far = turned(place, blocks)

time: 185 us -> 180 us (0.973)
  Pallas kernels: 11.8 us -> 8.23 us
  blocking collectives: 52.5 us -> 50.6 us
    pallas_call x1, Pallas kernels: 4.96 us -> 2.8 us  [turned(): pl.pallas_call(turn_kernel, grid_spec=pltpu.PrefetchScalarGridSpec(num_sc...]
    all_gather x3, blocking collectives: 16.3 us -> 14.3 us  [halved(): lax.all_gather(sent, axis)]
  transfers between devices with their start and end apart: 10 -> 10, of which waited for: 7 -> 7; matrix products, arithmetic and copies ran while one was open for 3% -> 4% of each run, Pallas kernels for 3% -> 2%
where the time goes in v3:
time: 180 us; the launch traced here: 177 us
  waiting for transfers between devices  58.6 us (33%)
  blocking collectives  50.6 us (28%)
  starting transfers between devices  50.3 us (28%)
  Pallas kernels  8.23 us (5%)
  other arithmetic  5.31 us (3%)
  matrix products  2.06 us (1%)
    all_to_all x1, waiting for transfers between devices, shards(): lax.all_to_all(split_columns(tokens, lax.axis_size(Y)), Y, 0, 0, tiled=True)  35.4 us
    all_gather x1, blocking collectives, replica_mean(): lax.all_gather(mean, ('xl', 'z0', 'core'), axis=0, tiled=True)  18.2 us
    all_gather x1, blocking collectives, shards(): near = lax.all_gather(residual, 'yh', axis=0, tiled=True)  18.1 us
    all_gather x3, blocking collectives, halved(): lax.all_gather(sent, axis)  14.3 us
    ppermute x1, starting transfers between devices, replica_mean(): back2 = lax.ppermute(own, 'z2', [(0, 2), (1, 0), (2, 1)])  12.4 us
    ppermute x2, starting transfers between devices, shards(): got.append(lax.ppermute(sent, 'xh', SWAP))  8.85 us
    ppermute x1, waiting for transfers between devices, shards(): other_rows = lax.ppermute(weight_rows, 'xh', SWAP)  7.81 us
    all_to_all x1, starting transfers between devices, shards(): lax.all_to_all(split_columns(tokens, lax.axis_size(Y)), Y, 0, 0, tiled=True)  7.78 us
  transfers between devices with their start and end apart: 10, of which 7 were waited for; matrix products, arithmetic and copies ran while one was open for 4% of the time, Pallas kernels for 2%

profile of v3, /device:TPU:1, one launch (start us, length us, event | category | flops | bytes accessed | tf_op | source)
XLA Modules:
  0.0 177.2 jit_solution(8430252748489473707)
XLA Ops:
  0.6 2.4 %split_columns.1 = bf16[8,128,1024]{2,1,0:T(8,128)(2,1)} custom-call(bf16[128,8192]{1,0:T(8,128)(2,1)} %tokens_ref.1), custom_call_target="tpu_custom_call" | custom-call | tf_op jit(solution)/shard_map/split_columns/pallas_call | solution.py:75
  3.1 7.8 %all-to-all-start = ((bf16[8,128,1024]{2,1,0:T(8,128)(2,1)}), bf16[8,128,1024]{2,1,0:T(8,128)(2,1)S(1)}, u32[]{:S(2)}, u32[]{:S(2)}) async-start(bf16[8,128,1024]{2,1,0:T(8,128)(2,1)} %split_columns.1), calls=%async_computation | async-start | bytes 4194304 | tf_op jit(solution)/shard_map/all_to_all | solution.py:191
  10.8 4.7 %collective-permute-start.3 = (bf16[512,512]{1,0:T(8,128)(2,1)S(1)}, bf16[512,512]{1,0:T(8,128)(2,1)S(1)}, u32[]{:S(2)}, u32[]{:S(2)}) collective-permute-start(bf16[512,512]{1,0:T(8,128)(2,1)S(1)} %bitcast.29), channel_id=1, source_target_pairs={{0,1},{1,0},{2,3},{3,2},{4,5},{5,4},{6,7},{7,6},{8,9},{9,8},{10,11... | collective-permute-start | bytes 1572872 | tf_op jit(solution)/shard_map/ppermute | solution.py:193
  15.5 7.8 %collective-permute-done.3 = bf16[512,512]{1,0:T(8,128)(2,1)S(1)} collective-permute-done((bf16[512,512]{1,0:T(8,128)(2,1)S(1)}, bf16[512,512]{1,0:T(8,128)(2,1)S(1)}, u32[]{:S(2)}, u32[]{:S(2)}) %collective-permute-start.3) | collective-permute-done | bytes 524320 | tf_op jit(solution)/shard_map/ppermute | solution.py:193
  23.5 35.4 %all-to-all-done.near_ref.far_ref.x_ref = bf16[8,128,1024]{2,1,0:T(8,128)(2,1)S(1)} async-done(((bf16[8,128,1024]{2,1,0:T(8,128)(2,1)}), bf16[8,128,1024]{2,1,0:T(8,128)(2,1)S(1)}, u32[]{:S(2)}, u32[]{:S(2)}) %all-to-all-start) | async-done | bytes 2097184 | tf_op jit(solution)/shard_map/all_to_all | solution.py:191
  58.9 2.2 %partial_keys.1 = bf16[8,128,512]{2,1,0:T(8,128)(2,1)} custom-call(bf16[8,128,1024]{2,1,0:T(8,128)(2,1)S(1)} %all-to-all-done.near_ref.far_ref.x_ref, bf16[1024,512]{1,0:T(8,128)(2,1)S(1)} %pad_maximum_fusion.rows_ref), custom_call_target="tpu_custom_call" | custom-call | flops 1073741824 | bytes 4194304 | tf_op jit(solution)/shard_map/partial_keys/pallas_call | solution.py:100
  61.1 3.6 %all-to-all-start.1 = ((bf16[8,128,512]{2,1,0:T(8,128)(2,1)}), bf16[8,128,512]{2,1,0:T(8,128)(2,1)S(1)}, u32[]{:S(2)}, u32[]{:S(2)}) async-start(bf16[8,128,512]{2,1,0:T(8,128)(2,1)} %partial_keys.1), calls=%async_computation.1 | async-start | bytes 2097152 | tf_op jit(solution)/shard_map/all_to_all | solution.py:201
  64.7 1.1 dynamic-slice_convert_fusion
  65.8 4.3 %all-gather = bf16[4,2,1,64,512]{4,3,2,1,0:T(8,128)(2,1)S(1)} all-gather(bf16[2,2,1,64,512]{4,3,2,1,0:T(8,128)(2,1)S(1)} %dynamic-slice_convert_fusion), channel_id=2, replica_groups=mesh['xl'=2,'z2'=3,'z1'=2,'z0'=2,'core'=2,'yh'=4,'yl'=2,'xh'=2] {'core'}, dimensions={0}, use_global_device_ids=true | all-gather | bytes 786432 | tf_op jit(solution)/shard_map/all_gather | solution.py:27
  70.1 1.1 convert_add_fusion
  71.2 5.3 %all_gather.19 = bf16[2,2,64,512]{3,2,1,0:T(8,128)(2,1)S(1)} all-gather(bf16[1,2,64,512]{3,2,1,0:T(8,128)(2,1)S(1)} %dynamic-slice_convert_fusion.1), channel_id=1, replica_groups=mesh['xl'=2,'z2'=3,'z1'=2,'z0'=2,'core'=2,'yh'=4,'yl'=2,'xh'=2] {'xl'}, dimensions={0}, use_global_device_ids=true | all-gather | bytes 393216 | tf_op jit(solution)/shard_map/all_gather | solution.py:27
  76.6 4.7 %all-gather.1 = bf16[2,1,64,512]{3,2,1,0:T(8,128)(2,1)S(1)} all-gather(bf16[1,1,64,512]{3,2,1,0:T(8,128)(2,1)S(1)} %dynamic-slice_convert_fusion.2), channel_id=3, replica_groups=mesh['xl'=2,'z2'=3,'z1'=2,'z0'=2,'core'=2,'yh'=4,'yl'=2,'xh'=2] {'z0'}, dimensions={0}, use_global_device_ids=true | all-gather | bytes 196608 | tf_op jit(solution)/shard_map/all_gather | solution.py:27
  81.4 5.8 %collective-permute-start = (bf16[64,512]{1,0:T(8,128)(2,1)S(1)}, bf16[64,512]{1,0:T(8,128)(2,1)S(1)}, u32[]{:S(2)}, u32[]{:S(2)}) collective-permute-start(bf16[64,512]{1,0:T(8,128)(2,1)S(1)} %fusion.8), channel_id=1, source_target_pairs={{0,64},{64,0},{1,65},{65,1},{2,66},{66,2},{3,67},{67,3},{4,68},{68... | collective-permute-start | bytes 196616 | tf_op jit(solution)/shard_map/ppermute | solution.py:39
  87.2 1.6 collective-permute-done
  88.8 12.4 %collective-permute-start.2 = (bf16[64,512]{1,0:T(8,128)(2,1)S(1)}, bf16[64,512]{1,0:T(8,128)(2,1)S(1)}, u32[]{:S(2)}, u32[]{:S(2)}) collective-permute-start(bf16[64,512]{1,0:T(8,128)(2,1)S(1)} %add_convert_fusion.1), channel_id=1, source_target_pairs={{0,256},{128,0},{256,128},{1,257},{129,1},{257,129},{2,258},{130,2... | collective-permute-start | bytes 196616 | tf_op jit(solution)/shard_map/ppermute | solution.py:42
  101.2 1.9 %collective-permute-start.1 = (bf16[64,512]{1,0:T(8,128)(2,1)S(1)}, bf16[64,512]{1,0:T(8,128)(2,1)S(1)}, u32[]{:S(2)}, u32[]{:S(2)}) collective-permute-start(bf16[64,512]{1,0:T(8,128)(2,1)S(1)} %add_convert_fusion.1), channel_id=1, source_target_pairs={{0,128},{128,256},{256,0},{1,129},{129,257},{257,1},{2,130},{130,2... | collective-permute-start | bytes 196616 | tf_op jit(solution)/shard_map/ppermute | solution.py:41
  103.3 7.1 %collective-permute-done.1 = bf16[64,512]{1,0:T(8,128)(2,1)S(1)} collective-permute-done((bf16[64,512]{1,0:T(8,128)(2,1)S(1)}, bf16[64,512]{1,0:T(8,128)(2,1)S(1)}, u32[]{:S(2)}, u32[]{:S(2)}) %collective-permute-start.1) | collective-permute-done | bytes 65568 | tf_op jit(solution)/shard_map/ppermute | solution.py:41
  110.4 18.2 %all_gather.21 = bf16[512,512]{1,0:T(8,128)(2,1)S(1)} all-gather(bf16[64,512]{1,0:T(8,128)(2,1)S(1)} %multiply_convert_fusion), channel_id=1, replica_groups=mesh['xl'=2,'z2'=3,'z1'=2,'z0'=2,'core'=2,'yh'=4,'yl'=2,'xh'=2] {'xl','z..., dimensions={0}, use_global_device_ids=true | all-gather | bytes 589824 | tf_op jit(solution)/shard_map/all_gather | solution.py:50
  128.6 1.1 convert_element_type.108
  129.7 2.8 %turn.1 = (bf16[512,512]{1,0:T(8,128)(2,1)}, bf16[512,512]{1,0:T(8,128)(2,1)}, bf16[512,512]{1,0:T(8,128)(2,1)}, bf16[512,512]{1,0:T(8,128)(2,1)}) custom-call(s32[2]{0:T(128)S(1)} %pad_add_fusion.place_ref, bf16[8,128,1024]{2,1,0:T(8,128)(2,1)S(1)} %all-to-all-done.near_ref.far_ref.x_ref, bf16[8,128,1024]{2,1,0:T(8,128)(2,1)S(1)} %all-to-all-done.near_ref.far_ref.x_ref), custom_call_target="tpu_custom_call" | custom-call | bytes 4194304 | tf_op jit(solution)/shard_map/turn/pallas_call | solution.py:140
  132.5 0.8 residual.1
  133.3 18.1 %all_gather.22 = bf16[512,512]{1,0:T(8,128)(2,1)S(1)} all-gather(bf16[128,512]{1,0:T(8,128)(2,1)} %residual.1), channel_id=1, replica_groups=mesh['xl'=2,'z2'=3,'z1'=2,'z0'=2,'core'=2,'yh'=4,'yl'=2,'xh'=2] {'yh'}, dimensions={0}, use_global_device_ids=true | all-gather | bytes 655360 | tf_op jit(solution)/shard_map/all_gather | solution.py:205
  151.4 0.4 fusion.11
  151.9 1.9 %collective-permute-start.5 = (bf16[512,256]{1,0:T(8,128)(2,1)S(1)}, bf16[512,256]{1,0:T(8,128)(2,1)S(1)}, u32[]{:S(2)}, u32[]{:S(2)}) collective-permute-start(bf16[512,256]{1,0:T(8,128)(2,1)S(1)} %get-tuple-element.19), channel_id=1, source_target_pairs={{0,2},{2,0},{1,3},{3,1},{4,6},{6,4},{5,7},{7,5},{8,10},{10,8},{9,1... | collective-permute-start | bytes 786440 | tf_op jit(solution)/shard_map/ppermute | solution.py:209
  153.8 3.4 %collective-permute-start.4 = (bf16[512,256]{1,0:T(8,128)(2,1)S(1)}, bf16[512,256]{1,0:T(8,128)(2,1)S(1)}, u32[]{:S(2)}, u32[]{:S(2)}) collective-permute-start(bf16[512,256]{1,0:T(8,128)(2,1)S(1)} %get-tuple-element.20), channel_id=1, source_target_pairs={{0,2},{2,0},{1,3},{3,1},{4,6},{6,4},{5,7},{7,5},{8,10},{10,8},{9,1... | collective-permute-start | bytes 786440 | tf_op jit(solution)/shard_map/ppermute | solution.py:209
  157.6 1.3 collective-permute-done.5
  159.3 4.4 %collective-permute-start.6 = (bf16[512,256]{1,0:T(8,128)(2,1)S(1)}, bf16[512,256]{1,0:T(8,128)(2,1)S(1)}, u32[]{:S(2)}, u32[]{:S(2)}) collective-permute-start(bf16[512,256]{1,0:T(8,128)(2,1)S(1)} %fusion.7), channel_id=1, source_target_pairs={{0,1},{1,0},{2,3},{3,2},{4,5},{5,4},{6,7},{7,6},{8,9},{9,8},{10,11... | collective-permute-start | bytes 786440 | tf_op jit(solution)/shard_map/ppermute | solution.py:220
  163.7 1.2 collective-permute-done.4
  165.2 4.5 %collective-permute-start.7 = (bf16[512,256]{1,0:T(8,128)(2,1)S(1)}, bf16[512,256]{1,0:T(8,128)(2,1)S(1)}, u32[]{:S(2)}, u32[]{:S(2)}) collective-permute-start(bf16[512,256]{1,0:T(8,128)(2,1)S(1)} %fusion.6), channel_id=1, source_target_pairs={{0,1},{1,0},{2,3},{3,2},{4,5},{5,4},{6,7},{7,6},{8,9},{9,8},{10,11... | collective-permute-start | bytes 786440 | tf_op jit(solution)/shard_map/ppermute | solution.py:220
  169.7 1.7 add_multiply_fusion
  172.2 4.1 %collective-permute-done.7 = bf16[512,256]{1,0:T(8,128)(2,1)S(1)} collective-permute-done((bf16[512,256]{1,0:T(8,128)(2,1)S(1)}, bf16[512,256]{1,0:T(8,128)(2,1)S(1)}, u32[]{:S(2)}, u32[]{:S(2)}) %collective-permute-start.7) | collective-permute-done | bytes 262176 | tf_op jit(solution)/shard_map/ppermute | solution.py:220
  176.4 0.8 maximum_bitcast_fusion
  (40 shorter events, 2.3 us)
Async XLA Ops:
  3.0 7.8 %copy-start.3 = (bf16[1,512,512]{2,1,0:T(8,128)(2,1)S(1)}, bf16[1,512,512]{2,1,0:T(8,128)(2,1)}, u32[]{:S(2)}) copy-start(bf16[1,512,512]{2,1,0:T(8,128)(2,1)} %param.8) | copy-start | bytes 1572868
  3.1 55.9 %all-to-all-start = ((bf16[8,128,1024]{2,1,0:T(8,128)(2,1)}), bf16[8,128,1024]{2,1,0:T(8,128)(2,1)S(1)}, u32[]{:S(2)}, u32[]{:S(2)}) async-start(bf16[8,128,1024]{2,1,0:T(8,128)(2,1)} %split_columns.1), calls=%async_computation | async-start | bytes 4194304 | tf_op jit(solution)/shard_map/all_to_all | solution.py:191
  10.8 12.5 %collective-permute-start.3 = (bf16[512,512]{1,0:T(8,128)(2,1)S(1)}, bf16[512,512]{1,0:T(8,128)(2,1)S(1)}, u32[]{:S(2)}, u32[]{:S(2)}) collective-permute-start(bf16[512,512]{1,0:T(8,128)(2,1)S(1)} %bitcast.29), channel_id=1, source_target_pairs={{0,1},{1,0},{2,3},{3,2},{4,5},{5,4},{6,7},{7,6},{8,9},{9,8},{10,11... | collective-permute-start | bytes 1572872 | tf_op jit(solution)/shard_map/ppermute | solution.py:193
  61.1 71.3 %all-to-all-start.1 = ((bf16[8,128,512]{2,1,0:T(8,128)(2,1)}), bf16[8,128,512]{2,1,0:T(8,128)(2,1)S(1)}, u32[]{:S(2)}, u32[]{:S(2)}) async-start(bf16[8,128,512]{2,1,0:T(8,128)(2,1)} %partial_keys.1), calls=%async_computation.1 | async-start | bytes 2097152 | tf_op jit(solution)/shard_map/all_to_all | solution.py:201
  81.4 7.5 %collective-permute-start = (bf16[64,512]{1,0:T(8,128)(2,1)S(1)}, bf16[64,512]{1,0:T(8,128)(2,1)S(1)}, u32[]{:S(2)}, u32[]{:S(2)}) collective-permute-start(bf16[64,512]{1,0:T(8,128)(2,1)S(1)} %fusion.8), channel_id=1, source_target_pairs={{0,64},{64,0},{1,65},{65,1},{2,66},{66,2},{3,67},{67,3},{4,68},{68... | collective-permute-start | bytes 196616 | tf_op jit(solution)/shard_map/ppermute | solution.py:39
  88.8 14.4 %collective-permute-start.2 = (bf16[64,512]{1,0:T(8,128)(2,1)S(1)}, bf16[64,512]{1,0:T(8,128)(2,1)S(1)}, u32[]{:S(2)}, u32[]{:S(2)}) collective-permute-start(bf16[64,512]{1,0:T(8,128)(2,1)S(1)} %add_convert_fusion.1), channel_id=1, source_target_pairs={{0,256},{128,0},{256,128},{1,257},{129,1},{257,129},{2,258},{130,2... | collective-permute-start | bytes 196616 | tf_op jit(solution)/shard_map/ppermute | solution.py:42
  101.2 9.1 %collective-permute-start.1 = (bf16[64,512]{1,0:T(8,128)(2,1)S(1)}, bf16[64,512]{1,0:T(8,128)(2,1)S(1)}, u32[]{:S(2)}, u32[]{:S(2)}) collective-permute-start(bf16[64,512]{1,0:T(8,128)(2,1)S(1)} %add_convert_fusion.1), channel_id=1, source_target_pairs={{0,128},{128,256},{256,0},{1,129},{129,257},{257,1},{2,130},{130,2... | collective-permute-start | bytes 196616 | tf_op jit(solution)/shard_map/ppermute | solution.py:41
  129.7 2.8 %copy-start = (bf16[128,512]{1,0:T(8,128)(2,1)S(1)}, bf16[128,512]{1,0:T(8,128)(2,1)}, u32[]{:S(2)}) copy-start(bf16[128,512]{1,0:T(8,128)(2,1)} %target_ref.1) | copy-start | bytes 393220
  132.5 18.9 %copy-start.9 = (bf16[512,512]{1,0:T(8,128)(2,1)S(1)}, bf16[512,512]{1,0:T(8,128)(2,1)}, u32[]{:S(2)}) copy-start(bf16[512,512]{1,0:T(8,128)(2,1)} %get-tuple-element.12) | copy-start | bytes 1572868
  133.3 23.9 %copy-start.8 = (bf16[512,512]{1,0:T(8,128)(2,1)S(1)}, bf16[512,512]{1,0:T(8,128)(2,1)}, u32[]{:S(2)}) copy-start(bf16[512,512]{1,0:T(8,128)(2,1)} %get-tuple-element.9) | copy-start | bytes 1572868
  151.4 7.6 %copy-start.2 = (bf16[512,512]{1,0:T(8,128)(2,1)S(1)}, bf16[512,512]{1,0:T(8,128)(2,1)}, u32[]{:S(2)}) copy-start(bf16[512,512]{1,0:T(8,128)(2,1)} %get-tuple-element.10) | copy-start | bytes 1572868
  151.9 7.1 %collective-permute-start.5 = (bf16[512,256]{1,0:T(8,128)(2,1)S(1)}, bf16[512,256]{1,0:T(8,128)(2,1)S(1)}, u32[]{:S(2)}, u32[]{:S(2)}) collective-permute-start(bf16[512,256]{1,0:T(8,128)(2,1)S(1)} %get-tuple-element.19), channel_id=1, source_target_pairs={{0,2},{2,0},{1,3},{3,1},{4,6},{6,4},{5,7},{7,5},{8,10},{10,8},{9,1... | collective-permute-start | bytes 786440 | tf_op jit(solution)/shard_map/ppermute | solution.py:209
  153.8 11.1 %collective-permute-start.4 = (bf16[512,256]{1,0:T(8,128)(2,1)S(1)}, bf16[512,256]{1,0:T(8,128)(2,1)S(1)}, u32[]{:S(2)}, u32[]{:S(2)}) collective-permute-start(bf16[512,256]{1,0:T(8,128)(2,1)S(1)} %get-tuple-element.20), channel_id=1, source_target_pairs={{0,2},{2,0},{1,3},{3,1},{4,6},{6,4},{5,7},{7,5},{8,10},{10,8},{9,1... | collective-permute-start | bytes 786440 | tf_op jit(solution)/shard_map/ppermute | solution.py:209
  157.2 12.5 %copy-start.7 = (f32[512,512]{1,0:T(8,128)S(1)}, f32[512,512]{1,0:T(8,128)}, u32[]{:S(2)}) copy-start(f32[512,512]{1,0:T(8,128)} %param.11) | copy-start | bytes 3145732
  157.6 12.1 %copy-start.1 = (f32[512,512]{1,0:T(8,128)S(1)}, f32[512,512]{1,0:T(8,128)}, u32[]{:S(2)}) copy-start(f32[512,512]{1,0:T(8,128)} %convert_element_type.108) | copy-start | bytes 3145732
  157.6 12.1 %copy-start.4 = (bf16[1,512,512]{2,1,0:T(8,128)(2,1)S(1)}, bf16[1,512,512]{2,1,0:T(8,128)(2,1)}, u32[]{:S(2)}) copy-start(bf16[1,512,512]{2,1,0:T(8,128)(2,1)} %param.8) | copy-start | bytes 1572868
  157.6 12.1 %copy-start.6 = (f32[512,512]{1,0:T(8,128)S(1)}, f32[512,512]{1,0:T(8,128)}, u32[]{:S(2)}) copy-start(f32[512,512]{1,0:T(8,128)} %param.10) | copy-start | bytes 3145732
  159.3 12.8 %collective-permute-start.6 = (bf16[512,256]{1,0:T(8,128)(2,1)S(1)}, bf16[512,256]{1,0:T(8,128)(2,1)S(1)}, u32[]{:S(2)}, u32[]{:S(2)}) collective-permute-start(bf16[512,256]{1,0:T(8,128)(2,1)S(1)} %fusion.7), channel_id=1, source_target_pairs={{0,1},{1,0},{2,3},{3,2},{4,5},{5,4},{6,7},{7,6},{8,9},{9,8},{10,11... | collective-permute-start | bytes 786440 | tf_op jit(solution)/shard_map/ppermute | solution.py:220
  165.2 6.3 %copy-start.5 = (bf16[512,512]{1,0:T(8,128)(2,1)S(1)}, bf16[512,512]{1,0:T(8,128)(2,1)}, u32[]{:S(2)}) copy-start(bf16[512,512]{1,0:T(8,128)(2,1)} %get-tuple-element.13) | copy-start | bytes 1572868
  165.2 11.1 %collective-permute-start.7 = (bf16[512,256]{1,0:T(8,128)(2,1)S(1)}, bf16[512,256]{1,0:T(8,128)(2,1)S(1)}, u32[]{:S(2)}, u32[]{:S(2)}) collective-permute-start(bf16[512,256]{1,0:T(8,128)(2,1)S(1)} %fusion.6), channel_id=1, source_target_pairs={{0,1},{1,0},{2,3},{3,2},{4,5},{5,4},{6,7},{7,6},{8,9},{9,8},{10,11... | collective-permute-start | bytes 786440 | tf_op jit(solution)/shard_map/ppermute | solution.py:220

commit v4 on v3

--- a/solution.py
+++ b/solution.py
@@ -87,9 +87,10 @@
 
 
 def partial_kernel(scale, x_ref, rows_ref, out_ref):
-    parts, rows, columns = x_ref.shape
+    parts, rows, _ = out_ref.shape
+    block = x_ref[pl.ds(pl.program_id(0) * parts, parts)]
     total = jnp.dot(
-        x_ref[...].reshape(parts * rows, columns), rows_ref[...], preferred_element_type=jnp.float32
+        block.reshape(parts * rows, x_ref.shape[2]), rows_ref[...], preferred_element_type=jnp.float32
     )
     out_ref[...] = (total * scale).astype(out_ref.dtype).reshape(out_ref.shape)
 
@@ -100,10 +101,7 @@
     return pl.pallas_call(
         functools.partial(partial_kernel, scale),
         grid=(2,),
-        in_specs=[
-            pl.BlockSpec((parts // 2, rows, columns), lambda i: (i, 0, 0)),
-            pl.BlockSpec((columns, key_width), lambda i: (0, 0)),
-        ],
+        in_specs=[pl.BlockSpec(memory_space=pltpu.VMEM)] * 2,
         out_specs=pl.BlockSpec((parts // 2, rows, key_width), lambda i: (i, 0, 0)),
         out_shape=pltpu.HBM((parts, rows, key_width), jnp.bfloat16),
         compiler_params=pltpu.CompilerParams(vmem_limit_bytes=VMEM_LIMIT),

time: 180 us -> 180 us (level)
  no operation moved by 1% of the time
where the time goes in v4:
time: 180 us; the launch traced here: 177 us
  waiting for transfers between devices  58.6 us (33%)
  blocking collectives  50.6 us (28%)
  starting transfers between devices  50.3 us (28%)
  Pallas kernels  8.23 us (5%)
  other arithmetic  5.31 us (3%)
  matrix products  2.06 us (1%)
    all_to_all x1, waiting for transfers between devices, shards(): lax.all_to_all(split_columns(tokens, lax.axis_size(Y)), Y, 0, 0, tiled=True)  35.4 us
    all_gather x1, blocking collectives, replica_mean(): lax.all_gather(mean, ('xl', 'z0', 'core'), axis=0, tiled=True)  18.2 us
    all_gather x1, blocking collectives, shards(): near = lax.all_gather(residual, 'yh', axis=0, tiled=True)  18.1 us
    all_gather x3, blocking collectives, halved(): lax.all_gather(sent, axis)  14.3 us
    ppermute x1, starting transfers between devices, replica_mean(): back2 = lax.ppermute(own, 'z2', [(0, 2), (1, 0), (2, 1)])  12.4 us
    ppermute x2, starting transfers between devices, shards(): got.append(lax.ppermute(sent, 'xh', SWAP))  8.85 us
    ppermute x1, waiting for transfers between devices, shards(): other_rows = lax.ppermute(weight_rows, 'xh', SWAP)  7.81 us
    all_to_all x1, starting transfers between devices, shards(): lax.all_to_all(split_columns(tokens, lax.axis_size(Y)), Y, 0, 0, tiled=True)  7.78 us
  transfers between devices with their start and end apart: 10, of which 7 were waited for; matrix products, arithmetic and copies ran while one was open for 4% of the time, Pallas kernels for 2%

profile of v4, /device:TPU:1, one launch (start us, length us, event | category | flops | bytes accessed | tf_op | source)
XLA Modules:
  0.0 177.2 jit_solution(17988122278883137387)
XLA Ops:
  0.6 2.4 %split_columns.1 = bf16[8,128,1024]{2,1,0:T(8,128)(2,1)} custom-call(bf16[128,8192]{1,0:T(8,128)(2,1)} %tokens_ref.1), custom_call_target="tpu_custom_call" | custom-call | tf_op jit(solution)/shard_map/split_columns/pallas_call | solution.py:75
  3.1 7.8 %all-to-all-start = ((bf16[8,128,1024]{2,1,0:T(8,128)(2,1)}), bf16[8,128,1024]{2,1,0:T(8,128)(2,1)S(1)}, u32[]{:S(2)}, u32[]{:S(2)}) async-start(bf16[8,128,1024]{2,1,0:T(8,128)(2,1)} %split_columns.1), calls=%async_computation | async-start | bytes 4194304 | tf_op jit(solution)/shard_map/all_to_all | solution.py:189
  10.8 4.7 %collective-permute-start.3 = (bf16[512,512]{1,0:T(8,128)(2,1)S(1)}, bf16[512,512]{1,0:T(8,128)(2,1)S(1)}, u32[]{:S(2)}, u32[]{:S(2)}) collective-permute-start(bf16[512,512]{1,0:T(8,128)(2,1)S(1)} %bitcast.29), channel_id=1, source_target_pairs={{0,1},{1,0},{2,3},{3,2},{4,5},{5,4},{6,7},{7,6},{8,9},{9,8},{10,11... | collective-permute-start | bytes 1572872 | tf_op jit(solution)/shard_map/ppermute | solution.py:191
  15.5 7.8 %collective-permute-done.3 = bf16[512,512]{1,0:T(8,128)(2,1)S(1)} collective-permute-done((bf16[512,512]{1,0:T(8,128)(2,1)S(1)}, bf16[512,512]{1,0:T(8,128)(2,1)S(1)}, u32[]{:S(2)}, u32[]{:S(2)}) %collective-permute-start.3) | collective-permute-done | bytes 524320 | tf_op jit(solution)/shard_map/ppermute | solution.py:191
  23.5 35.4 %all-to-all-done.near_ref.far_ref.x_ref = bf16[8,128,1024]{2,1,0:T(8,128)(2,1)S(1)} async-done(((bf16[8,128,1024]{2,1,0:T(8,128)(2,1)}), bf16[8,128,1024]{2,1,0:T(8,128)(2,1)S(1)}, u32[]{:S(2)}, u32[]{:S(2)}) %all-to-all-start) | async-done | bytes 2097184 | tf_op jit(solution)/shard_map/all_to_all | solution.py:189
  58.9 2.2 %partial_keys.1 = bf16[8,128,512]{2,1,0:T(8,128)(2,1)} custom-call(bf16[8,128,1024]{2,1,0:T(8,128)(2,1)S(1)} %all-to-all-done.near_ref.far_ref.x_ref, bf16[1024,512]{1,0:T(8,128)(2,1)S(1)} %pad_maximum_fusion.rows_ref), custom_call_target="tpu_custom_call" | custom-call | flops 1073741824 | bytes 4194304 | tf_op jit(solution)/shard_map/partial_keys/pallas_call | solution.py:101
  61.1 3.6 %all-to-all-start.1 = ((bf16[8,128,512]{2,1,0:T(8,128)(2,1)}), bf16[8,128,512]{2,1,0:T(8,128)(2,1)S(1)}, u32[]{:S(2)}, u32[]{:S(2)}) async-start(bf16[8,128,512]{2,1,0:T(8,128)(2,1)} %partial_keys.1), calls=%async_computation.1 | async-start | bytes 2097152 | tf_op jit(solution)/shard_map/all_to_all | solution.py:199
  64.7 1.1 dynamic-slice_convert_fusion
  65.8 4.3 %all-gather = bf16[4,2,1,64,512]{4,3,2,1,0:T(8,128)(2,1)S(1)} all-gather(bf16[2,2,1,64,512]{4,3,2,1,0:T(8,128)(2,1)S(1)} %dynamic-slice_convert_fusion), channel_id=2, replica_groups=mesh['xl'=2,'z2'=3,'z1'=2,'z0'=2,'core'=2,'yh'=4,'yl'=2,'xh'=2] {'core'}, dimensions={0}, use_global_device_ids=true | all-gather | bytes 786432 | tf_op jit(solution)/shard_map/all_gather | solution.py:27
  70.1 1.1 convert_add_fusion
  71.2 5.3 %all_gather.19 = bf16[2,2,64,512]{3,2,1,0:T(8,128)(2,1)S(1)} all-gather(bf16[1,2,64,512]{3,2,1,0:T(8,128)(2,1)S(1)} %dynamic-slice_convert_fusion.1), channel_id=1, replica_groups=mesh['xl'=2,'z2'=3,'z1'=2,'z0'=2,'core'=2,'yh'=4,'yl'=2,'xh'=2] {'xl'}, dimensions={0}, use_global_device_ids=true | all-gather | bytes 393216 | tf_op jit(solution)/shard_map/all_gather | solution.py:27
  76.6 4.7 %all-gather.1 = bf16[2,1,64,512]{3,2,1,0:T(8,128)(2,1)S(1)} all-gather(bf16[1,1,64,512]{3,2,1,0:T(8,128)(2,1)S(1)} %dynamic-slice_convert_fusion.2), channel_id=3, replica_groups=mesh['xl'=2,'z2'=3,'z1'=2,'z0'=2,'core'=2,'yh'=4,'yl'=2,'xh'=2] {'z0'}, dimensions={0}, use_global_device_ids=true | all-gather | bytes 196608 | tf_op jit(solution)/shard_map/all_gather | solution.py:27
  81.4 5.8 %collective-permute-start = (bf16[64,512]{1,0:T(8,128)(2,1)S(1)}, bf16[64,512]{1,0:T(8,128)(2,1)S(1)}, u32[]{:S(2)}, u32[]{:S(2)}) collective-permute-start(bf16[64,512]{1,0:T(8,128)(2,1)S(1)} %fusion.8), channel_id=1, source_target_pairs={{0,64},{64,0},{1,65},{65,1},{2,66},{66,2},{3,67},{67,3},{4,68},{68... | collective-permute-start | bytes 196616 | tf_op jit(solution)/shard_map/ppermute | solution.py:39
  87.2 1.6 collective-permute-done
  88.8 12.4 %collective-permute-start.2 = (bf16[64,512]{1,0:T(8,128)(2,1)S(1)}, bf16[64,512]{1,0:T(8,128)(2,1)S(1)}, u32[]{:S(2)}, u32[]{:S(2)}) collective-permute-start(bf16[64,512]{1,0:T(8,128)(2,1)S(1)} %add_convert_fusion.1), channel_id=1, source_target_pairs={{0,256},{128,0},{256,128},{1,257},{129,1},{257,129},{2,258},{130,2... | collective-permute-start | bytes 196616 | tf_op jit(solution)/shard_map/ppermute | solution.py:42
  101.2 1.9 %collective-permute-start.1 = (bf16[64,512]{1,0:T(8,128)(2,1)S(1)}, bf16[64,512]{1,0:T(8,128)(2,1)S(1)}, u32[]{:S(2)}, u32[]{:S(2)}) collective-permute-start(bf16[64,512]{1,0:T(8,128)(2,1)S(1)} %add_convert_fusion.1), channel_id=1, source_target_pairs={{0,128},{128,256},{256,0},{1,129},{129,257},{257,1},{2,130},{130,2... | collective-permute-start | bytes 196616 | tf_op jit(solution)/shard_map/ppermute | solution.py:41
  103.3 7.1 %collective-permute-done.1 = bf16[64,512]{1,0:T(8,128)(2,1)S(1)} collective-permute-done((bf16[64,512]{1,0:T(8,128)(2,1)S(1)}, bf16[64,512]{1,0:T(8,128)(2,1)S(1)}, u32[]{:S(2)}, u32[]{:S(2)}) %collective-permute-start.1) | collective-permute-done | bytes 65568 | tf_op jit(solution)/shard_map/ppermute | solution.py:41
  110.4 18.2 %all_gather.21 = bf16[512,512]{1,0:T(8,128)(2,1)S(1)} all-gather(bf16[64,512]{1,0:T(8,128)(2,1)S(1)} %multiply_convert_fusion), channel_id=1, replica_groups=mesh['xl'=2,'z2'=3,'z1'=2,'z0'=2,'core'=2,'yh'=4,'yl'=2,'xh'=2] {'xl','z..., dimensions={0}, use_global_device_ids=true | all-gather | bytes 589824 | tf_op jit(solution)/shard_map/all_gather | solution.py:50
  128.6 1.1 convert_element_type.108
  129.7 2.8 %turn.1 = (bf16[512,512]{1,0:T(8,128)(2,1)}, bf16[512,512]{1,0:T(8,128)(2,1)}, bf16[512,512]{1,0:T(8,128)(2,1)}, bf16[512,512]{1,0:T(8,128)(2,1)}) custom-call(s32[2]{0:T(128)S(1)} %pad_add_fusion.place_ref, bf16[8,128,1024]{2,1,0:T(8,128)(2,1)S(1)} %all-to-all-done.near_ref.far_ref.x_ref, bf16[8,128,1024]{2,1,0:T(8,128)(2,1)S(1)} %all-to-all-done.near_ref.far_ref.x_ref), custom_call_target="tpu_custom_call" | custom-call | bytes 4194304 | tf_op jit(solution)/shard_map/turn/pallas_call | solution.py:138
  132.5 0.8 residual.1
  133.3 18.1 %all_gather.22 = bf16[512,512]{1,0:T(8,128)(2,1)S(1)} all-gather(bf16[128,512]{1,0:T(8,128)(2,1)} %residual.1), channel_id=1, replica_groups=mesh['xl'=2,'z2'=3,'z1'=2,'z0'=2,'core'=2,'yh'=4,'yl'=2,'xh'=2] {'yh'}, dimensions={0}, use_global_device_ids=true | all-gather | bytes 655360 | tf_op jit(solution)/shard_map/all_gather | solution.py:203
  151.4 0.4 fusion.11
  151.9 1.9 %collective-permute-start.5 = (bf16[512,256]{1,0:T(8,128)(2,1)S(1)}, bf16[512,256]{1,0:T(8,128)(2,1)S(1)}, u32[]{:S(2)}, u32[]{:S(2)}) collective-permute-start(bf16[512,256]{1,0:T(8,128)(2,1)S(1)} %get-tuple-element.19), channel_id=1, source_target_pairs={{0,2},{2,0},{1,3},{3,1},{4,6},{6,4},{5,7},{7,5},{8,10},{10,8},{9,1... | collective-permute-start | bytes 786440 | tf_op jit(solution)/shard_map/ppermute | solution.py:207
  153.8 3.4 %collective-permute-start.4 = (bf16[512,256]{1,0:T(8,128)(2,1)S(1)}, bf16[512,256]{1,0:T(8,128)(2,1)S(1)}, u32[]{:S(2)}, u32[]{:S(2)}) collective-permute-start(bf16[512,256]{1,0:T(8,128)(2,1)S(1)} %get-tuple-element.20), channel_id=1, source_target_pairs={{0,2},{2,0},{1,3},{3,1},{4,6},{6,4},{5,7},{7,5},{8,10},{10,8},{9,1... | collective-permute-start | bytes 786440 | tf_op jit(solution)/shard_map/ppermute | solution.py:207
  157.6 1.3 collective-permute-done.5
  159.3 4.4 %collective-permute-start.6 = (bf16[512,256]{1,0:T(8,128)(2,1)S(1)}, bf16[512,256]{1,0:T(8,128)(2,1)S(1)}, u32[]{:S(2)}, u32[]{:S(2)}) collective-permute-start(bf16[512,256]{1,0:T(8,128)(2,1)S(1)} %fusion.7), channel_id=1, source_target_pairs={{0,1},{1,0},{2,3},{3,2},{4,5},{5,4},{6,7},{7,6},{8,9},{9,8},{10,11... | collective-permute-start | bytes 786440 | tf_op jit(solution)/shard_map/ppermute | solution.py:218
  163.7 1.2 collective-permute-done.4
  165.2 4.5 %collective-permute-start.7 = (bf16[512,256]{1,0:T(8,128)(2,1)S(1)}, bf16[512,256]{1,0:T(8,128)(2,1)S(1)}, u32[]{:S(2)}, u32[]{:S(2)}) collective-permute-start(bf16[512,256]{1,0:T(8,128)(2,1)S(1)} %fusion.6), channel_id=1, source_target_pairs={{0,1},{1,0},{2,3},{3,2},{4,5},{5,4},{6,7},{7,6},{8,9},{9,8},{10,11... | collective-permute-start | bytes 786440 | tf_op jit(solution)/shard_map/ppermute | solution.py:218
  169.7 1.7 add_multiply_fusion
  172.2 4.1 %collective-permute-done.7 = bf16[512,256]{1,0:T(8,128)(2,1)S(1)} collective-permute-done((bf16[512,256]{1,0:T(8,128)(2,1)S(1)}, bf16[512,256]{1,0:T(8,128)(2,1)S(1)}, u32[]{:S(2)}, u32[]{:S(2)}) %collective-permute-start.7) | collective-permute-done | bytes 262176 | tf_op jit(solution)/shard_map/ppermute | solution.py:218
  176.4 0.8 maximum_bitcast_fusion
  (40 shorter events, 2.3 us)
Async XLA Ops:
  3.0 7.8 %copy-start.3 = (bf16[1,512,512]{2,1,0:T(8,128)(2,1)S(1)}, bf16[1,512,512]{2,1,0:T(8,128)(2,1)}, u32[]{:S(2)}) copy-start(bf16[1,512,512]{2,1,0:T(8,128)(2,1)} %param.8) | copy-start | bytes 1572868
  3.1 55.9 %all-to-all-start = ((bf16[8,128,1024]{2,1,0:T(8,128)(2,1)}), bf16[8,128,1024]{2,1,0:T(8,128)(2,1)S(1)}, u32[]{:S(2)}, u32[]{:S(2)}) async-start(bf16[8,128,1024]{2,1,0:T(8,128)(2,1)} %split_columns.1), calls=%async_computation | async-start | bytes 4194304 | tf_op jit(solution)/shard_map/all_to_all | solution.py:189
  10.8 12.5 %collective-permute-start.3 = (bf16[512,512]{1,0:T(8,128)(2,1)S(1)}, bf16[512,512]{1,0:T(8,128)(2,1)S(1)}, u32[]{:S(2)}, u32[]{:S(2)}) collective-permute-start(bf16[512,512]{1,0:T(8,128)(2,1)S(1)} %bitcast.29), channel_id=1, source_target_pairs={{0,1},{1,0},{2,3},{3,2},{4,5},{5,4},{6,7},{7,6},{8,9},{9,8},{10,11... | collective-permute-start | bytes 1572872 | tf_op jit(solution)/shard_map/ppermute | solution.py:191
  61.1 71.3 %all-to-all-start.1 = ((bf16[8,128,512]{2,1,0:T(8,128)(2,1)}), bf16[8,128,512]{2,1,0:T(8,128)(2,1)S(1)}, u32[]{:S(2)}, u32[]{:S(2)}) async-start(bf16[8,128,512]{2,1,0:T(8,128)(2,1)} %partial_keys.1), calls=%async_computation.1 | async-start | bytes 2097152 | tf_op jit(solution)/shard_map/all_to_all | solution.py:199
  81.4 7.5 %collective-permute-start = (bf16[64,512]{1,0:T(8,128)(2,1)S(1)}, bf16[64,512]{1,0:T(8,128)(2,1)S(1)}, u32[]{:S(2)}, u32[]{:S(2)}) collective-permute-start(bf16[64,512]{1,0:T(8,128)(2,1)S(1)} %fusion.8), channel_id=1, source_target_pairs={{0,64},{64,0},{1,65},{65,1},{2,66},{66,2},{3,67},{67,3},{4,68},{68... | collective-permute-start | bytes 196616 | tf_op jit(solution)/shard_map/ppermute | solution.py:39
  88.8 14.4 %collective-permute-start.2 = (bf16[64,512]{1,0:T(8,128)(2,1)S(1)}, bf16[64,512]{1,0:T(8,128)(2,1)S(1)}, u32[]{:S(2)}, u32[]{:S(2)}) collective-permute-start(bf16[64,512]{1,0:T(8,128)(2,1)S(1)} %add_convert_fusion.1), channel_id=1, source_target_pairs={{0,256},{128,0},{256,128},{1,257},{129,1},{257,129},{2,258},{130,2... | collective-permute-start | bytes 196616 | tf_op jit(solution)/shard_map/ppermute | solution.py:42
  101.2 9.1 %collective-permute-start.1 = (bf16[64,512]{1,0:T(8,128)(2,1)S(1)}, bf16[64,512]{1,0:T(8,128)(2,1)S(1)}, u32[]{:S(2)}, u32[]{:S(2)}) collective-permute-start(bf16[64,512]{1,0:T(8,128)(2,1)S(1)} %add_convert_fusion.1), channel_id=1, source_target_pairs={{0,128},{128,256},{256,0},{1,129},{129,257},{257,1},{2,130},{130,2... | collective-permute-start | bytes 196616 | tf_op jit(solution)/shard_map/ppermute | solution.py:41
  129.7 2.8 %copy-start = (bf16[128,512]{1,0:T(8,128)(2,1)S(1)}, bf16[128,512]{1,0:T(8,128)(2,1)}, u32[]{:S(2)}) copy-start(bf16[128,512]{1,0:T(8,128)(2,1)} %target_ref.1) | copy-start | bytes 393220
  132.5 18.9 %copy-start.9 = (bf16[512,512]{1,0:T(8,128)(2,1)S(1)}, bf16[512,512]{1,0:T(8,128)(2,1)}, u32[]{:S(2)}) copy-start(bf16[512,512]{1,0:T(8,128)(2,1)} %get-tuple-element.12) | copy-start | bytes 1572868
  133.3 23.9 %copy-start.8 = (bf16[512,512]{1,0:T(8,128)(2,1)S(1)}, bf16[512,512]{1,0:T(8,128)(2,1)}, u32[]{:S(2)}) copy-start(bf16[512,512]{1,0:T(8,128)(2,1)} %get-tuple-element.9) | copy-start | bytes 1572868
  151.4 7.6 %copy-start.2 = (bf16[512,512]{1,0:T(8,128)(2,1)S(1)}, bf16[512,512]{1,0:T(8,128)(2,1)}, u32[]{:S(2)}) copy-start(bf16[512,512]{1,0:T(8,128)(2,1)} %get-tuple-element.10) | copy-start | bytes 1572868
  151.9 7.1 %collective-permute-start.5 = (bf16[512,256]{1,0:T(8,128)(2,1)S(1)}, bf16[512,256]{1,0:T(8,128)(2,1)S(1)}, u32[]{:S(2)}, u32[]{:S(2)}) collective-permute-start(bf16[512,256]{1,0:T(8,128)(2,1)S(1)} %get-tuple-element.19), channel_id=1, source_target_pairs={{0,2},{2,0},{1,3},{3,1},{4,6},{6,4},{5,7},{7,5},{8,10},{10,8},{9,1... | collective-permute-start | bytes 786440 | tf_op jit(solution)/shard_map/ppermute | solution.py:207
  153.8 11.1 %collective-permute-start.4 = (bf16[512,256]{1,0:T(8,128)(2,1)S(1)}, bf16[512,256]{1,0:T(8,128)(2,1)S(1)}, u32[]{:S(2)}, u32[]{:S(2)}) collective-permute-start(bf16[512,256]{1,0:T(8,128)(2,1)S(1)} %get-tuple-element.20), channel_id=1, source_target_pairs={{0,2},{2,0},{1,3},{3,1},{4,6},{6,4},{5,7},{7,5},{8,10},{10,8},{9,1... | collective-permute-start | bytes 786440 | tf_op jit(solution)/shard_map/ppermute | solution.py:207
  157.2 12.5 %copy-start.7 = (f32[512,512]{1,0:T(8,128)S(1)}, f32[512,512]{1,0:T(8,128)}, u32[]{:S(2)}) copy-start(f32[512,512]{1,0:T(8,128)} %param.11) | copy-start | bytes 3145732
  157.6 12.1 %copy-start.1 = (f32[512,512]{1,0:T(8,128)S(1)}, f32[512,512]{1,0:T(8,128)}, u32[]{:S(2)}) copy-start(f32[512,512]{1,0:T(8,128)} %convert_element_type.108) | copy-start | bytes 3145732
  157.6 12.1 %copy-start.4 = (bf16[1,512,512]{2,1,0:T(8,128)(2,1)S(1)}, bf16[1,512,512]{2,1,0:T(8,128)(2,1)}, u32[]{:S(2)}) copy-start(bf16[1,512,512]{2,1,0:T(8,128)(2,1)} %param.8) | copy-start | bytes 1572868
  157.6 12.1 %copy-start.6 = (f32[512,512]{1,0:T(8,128)S(1)}, f32[512,512]{1,0:T(8,128)}, u32[]{:S(2)}) copy-start(f32[512,512]{1,0:T(8,128)} %param.10) | copy-start | bytes 3145732
  159.3 12.8 %collective-permute-start.6 = (bf16[512,256]{1,0:T(8,128)(2,1)S(1)}, bf16[512,256]{1,0:T(8,128)(2,1)S(1)}, u32[]{:S(2)}, u32[]{:S(2)}) collective-permute-start(bf16[512,256]{1,0:T(8,128)(2,1)S(1)} %fusion.7), channel_id=1, source_target_pairs={{0,1},{1,0},{2,3},{3,2},{4,5},{5,4},{6,7},{7,6},{8,9},{9,8},{10,11... | collective-permute-start | bytes 786440 | tf_op jit(solution)/shard_map/ppermute | solution.py:218
  165.2 6.3 %copy-start.5 = (bf16[512,512]{1,0:T(8,128)(2,1)S(1)}, bf16[512,512]{1,0:T(8,128)(2,1)}, u32[]{:S(2)}) copy-start(bf16[512,512]{1,0:T(8,128)(2,1)} %get-tuple-element.13) | copy-start | bytes 1572868
  165.2 11.1 %collective-permute-start.7 = (bf16[512,256]{1,0:T(8,128)(2,1)S(1)}, bf16[512,256]{1,0:T(8,128)(2,1)S(1)}, u32[]{:S(2)}, u32[]{:S(2)}) collective-permute-start(bf16[512,256]{1,0:T(8,128)(2,1)S(1)} %fusion.6), channel_id=1, source_target_pairs={{0,1},{1,0},{2,3},{3,2},{4,5},{5,4},{6,7},{7,6},{8,9},{9,8},{10,11... | collective-permute-start | bytes 786440 | tf_op jit(solution)/shard_map/ppermute | solution.py:218
